TPU v7x, 512 devices: a whole 4x8x8 slice. The times are simulated.
512 devices in a mesh: blk: 64 (over z_hi, y, core), rep: 8 (over z_lo, x).
Axes of the slice: x: 4, y: 8, z: 8 (z_hi: 4, z_lo: 2; z = z_hi * 2 + z_lo), core: 2. Of those that a mesh axis runs over, the one named last changes fastest.
Arguments:
- features: bfloat16 [32768, 128], P('blk'), may hold values from -6 to 6
- weight: bfloat16 [128, 256], replicated, may hold values from -0.5 to 0.5
- tile_vals: bfloat16 [64, 8, 8, 12, 128, 128], P('blk', 'rep'), may hold values from -0.0390625 to 0.0390625
- tile_pos: int32 [64, 8, 8, 12], P('blk', 'rep'), may hold values from 0 to 15, as said below
- tile_count: int32 [64, 8, 8], P('blk', 'rep'), may hold values from 1 to 12, as said below
- cotangent: bfloat16 [32768, 256], P(('blk', 'rep')), may hold values from -6 to 6
Outputs:
- activations: bfloat16 [32768, 256], P(('blk', 'rep'))
- feat_grad: bfloat16 [32768, 128], P(('blk', 'rep'))
- weight_grad: float32 [128, 256], replicated
Inputs may be any that keep to these rules, and one draw needn't show every extreme that they name: `tile_pos`: within one row group, copy and section the entries are distinct. `tile_count`: row group 0 has all 12 slots live in every copy and section.
All inputs are finite; a program needn't handle non-finite values.
Results may differ from a plain program's by a relative error of at most 0.014.
Values may be sent and summed in bfloat16 or wider, within the bound.
A program may use at most 128 MiB of HBM per device.

v0:
```python
import jax
import jax.numpy as jnp
from jax import lax
from jax.sharding import PartitionSpec as P


def passed_along(block, axis, distance):
    devices = range(lax.axis_size(axis))
    route = [((i - distance) % len(devices), i) for i in devices]
    return lax.ppermute(block, axis, route)


def gelu_tanh(value):
    return jax.nn.gelu(value, approximate=True)


def section_forward(tile_block, positions, live_count, current, blocks):
    tile_size = tile_block.shape[-1]
    columns = current.reshape(blocks, tile_size, current.shape[-1])
    picked = columns[positions % blocks]
    live_mask = (jnp.arange(tile_block.shape[0], dtype=jnp.int32) < live_count).astype(jnp.float32)
    product = jnp.einsum("tik,tkf->tif", tile_block, picked, preferred_element_type=jnp.float32)
    product = product * live_mask[:, None, None]
    placing = (
        (positions // blocks)[:, None] == jnp.arange(blocks, dtype=jnp.int32)[None, :]
    ).astype(jnp.float32)
    return jnp.einsum("tn,tif->nif", placing, product).reshape(
        blocks * tile_size, current.shape[-1]
    )


def section_backward(tile_block, positions, live_count, grad_rows, blocks):
    tile_size = tile_block.shape[-1]
    rows_view = grad_rows.reshape(blocks, tile_size, grad_rows.shape[-1])
    picked = rows_view[positions // blocks]
    live_mask = (jnp.arange(tile_block.shape[0], dtype=jnp.int32) < live_count).astype(jnp.float32)
    product = jnp.einsum("tki,tkf->tif", tile_block, picked, preferred_element_type=jnp.float32)
    product = product * live_mask[:, None, None]
    placing = (
        (positions % blocks)[:, None] == jnp.arange(blocks, dtype=jnp.int32)[None, :]
    ).astype(jnp.float32)
    return jnp.einsum("tn,tif->nif", placing, product).reshape(
        blocks * tile_size, grad_rows.shape[-1]
    )


def skew_forward(value, rep_index, rep_size):
    for bit_index in range((rep_size - 1).bit_length()):
        moved = passed_along(value, "blk", 1 << bit_index)
        value = jnp.where(jnp.right_shift(rep_index, bit_index) % 2 == 1, moved, value)
    return value


def skew_back(value, rep_index, rep_size):
    for bit_index in range((rep_size - 1).bit_length()):
        moved = passed_along(value, "blk", -(1 << bit_index))
        value = jnp.where(jnp.right_shift(rep_index, bit_index) % 2 == 1, moved, value)
    return value


def local(features, weight, tile_vals, tile_pos, tile_count, cotangent):
    rep_size = lax.axis_size("rep")
    rep_index = lax.axis_index("rep")
    local_tiles = tile_vals[0, 0]
    local_pos = tile_pos[0, 0]
    local_count = tile_count[0, 0]
    section_count = local_tiles.shape[0]
    tile_size = local_tiles.shape[-1]
    blocks = features.shape[0] // tile_size
    rows_share = features.shape[0] // rep_size
    row_start = rep_index * rows_share

    def section_terms(section, current):
        return section_forward(
            lax.dynamic_index_in_dim(local_tiles, section, 0, keepdims=False),
            lax.dynamic_index_in_dim(local_pos, section, 0, keepdims=False),
            lax.dynamic_index_in_dim(local_count, section, 0, keepdims=False),
            current,
            blocks,
        )

    hidden = jnp.dot(features, weight, preferred_element_type=jnp.float32).astype(jnp.bfloat16)
    seeded = skew_forward(hidden, rep_index, rep_size)
    zeros_total = jnp.zeros((features.shape[0], weight.shape[1]), jnp.float32)

    def one_step(section, state):
        current, total = state
        total = total + section_terms(section, current)
        current = passed_along(current, "blk", rep_size)
        return (current, total)

    current, total = lax.fori_loop(0, section_count - 1, one_step, (seeded, zeros_total))
    total = total + section_terms(section_count - 1, current)
    pre = lax.psum_scatter(total, "rep", scatter_dimension=0, tiled=True)
    outputs, pullback = jax.vjp(gelu_tanh, pre)
    activations = outputs.astype(jnp.bfloat16)
    pre_grad = pullback(cotangent.astype(jnp.float32))[0].astype(jnp.bfloat16)
    grad_rows = lax.all_gather(pre_grad, "rep", axis=0, tiled=True)

    def back_terms(section):
        return section_backward(
            lax.dynamic_index_in_dim(local_tiles, section, 0, keepdims=False),
            lax.dynamic_index_in_dim(local_pos, section, 0, keepdims=False),
            lax.dynamic_index_in_dim(local_count, section, 0, keepdims=False),
            grad_rows,
            blocks,
        )

    def back_step(section, carried):
        return passed_along(carried + back_terms(section), "blk", rep_size)

    carried = lax.fori_loop(0, section_count, back_step, zeros_total)
    carried = skew_back(carried, rep_index, rep_size)
    hidden_grad = lax.psum_scatter(carried, "rep", scatter_dimension=0, tiled=True).astype(
        jnp.bfloat16
    )
    feat_grad = lax.dot_general(
        hidden_grad, weight, (((1,), (1,)), ((), ())), preferred_element_type=jnp.float32
    ).astype(jnp.bfloat16)
    feat_rows = lax.dynamic_slice_in_dim(features, row_start, rows_share, 0)
    partial_grad = lax.dot_general(
        feat_rows, hidden_grad, (((0,), (0,)), ((), ())), preferred_element_type=jnp.float32
    )
    weight_grad = lax.psum(partial_grad, ("blk", "rep"))
    return (activations, feat_grad, weight_grad)


def solution(mesh):
    placed = (
        P("blk", None),
        P(),
        P("blk", "rep", None, None, None, None),
        P("blk", "rep", None, None),
        P("blk", "rep", None),
        P(("blk", "rep"), None),
    )
    return jax.shard_map(
        local,
        mesh=mesh,
        in_specs=placed,
        out_specs=(P(("blk", "rep"), None), P(("blk", "rep"), None), P()),
        check_vma=False,
    )
```

profile of v0, /device:TPU:1, one launch (start us, length us, event | category | flops | bytes accessed | tf_op | source)
XLA Modules:
  0.0 1005.6 jit_solution(1865556596306336657)
XLA Ops:
  9.1 4.6 collective-permute-start.2
  15.0 3.9 collective-permute-done.2
  18.9 1.9 collective-permute-start.3
  21.6 14.1 %collective-permute-done.3 = bf16[512,256]{1,0:T(8,128)(2,1)S(1)} collective-permute-done((bf16[512,256]{1,0:T(8,128)(2,1)S(1)}, bf16[512,256]{1,0:T(8,128)(2,1)S(1)}, u32[]{:S(2)}, u32[]{:S(2)}) %collective-permute-start.3) | collective-permute-done | bytes 262176 | tf_op jit(solution)/shard_map/ppermute | solution.py:10
  35.7 1.9 collective-permute-start.4
  38.4 12.9 %collective-permute-done.4 = bf16[512,256]{1,0:T(8,128)(2,1)S(1)} collective-permute-done((bf16[512,256]{1,0:T(8,128)(2,1)S(1)}, bf16[512,256]{1,0:T(8,128)(2,1)S(1)}, u32[]{:S(2)}, u32[]{:S(2)}) %collective-permute-start.4) | collective-permute-done | bytes 262176 | tf_op jit(solution)/shard_map/ppermute | solution.py:10
  51.4 140.1 %while.34 = (s32[]{:T(128)}, bf16[512,256]{1,0:T(8,128)(2,1)S(1)}, f32[512,256]{1,0:T(8,128)S(1)}, s32[8,12]{1,0:T(8,128)S(1)}, bf16[8,12,128,128]{3,2,1,0:T(8,1...) while((s32[]{:T(128)}, bf16[512,256]{1,0:T(8,128)(2,1)S(1)}, f32[512,256]{1,0:T(8,128)S(1)}, ...), condition=%wide.region_1.2_spmd.clone, body=%wide.region_0.1_spmd.clone.sunk | while | flops 104465824 | bytes 10621531 | solution.py:92
  51.4 1.9 collective-permute-start.1
  55.2 1.4 fusion.77
  57.8 10.0 collective-permute-done.1
  67.8 1.9 collective-permute-start.1
  74.2 13.7 %collective-permute-done.1 = bf16[512,256]{1,0:T(8,128)(2,1)S(1)} collective-permute-done((bf16[512,256]{1,0:T(8,128)(2,1)S(1)}, bf16[512,256]{1,0:T(8,128)(2,1)S(1)}, u32[]{:S(2)}, u32[]{:S(2)}) %collective-permute-start.1) | collective-permute-done | bytes 262176 | tf_op jit(solution)/shard_map/while/body/eval_jaxpr/ppermute | solution.py:10
  87.9 1.9 collective-permute-start.1
  94.3 14.5 %collective-permute-done.1 = bf16[512,256]{1,0:T(8,128)(2,1)S(1)} collective-permute-done((bf16[512,256]{1,0:T(8,128)(2,1)S(1)}, bf16[512,256]{1,0:T(8,128)(2,1)S(1)}, u32[]{:S(2)}, u32[]{:S(2)}) %collective-permute-start.1) | collective-permute-done | bytes 262176 | tf_op jit(solution)/shard_map/while/body/eval_jaxpr/ppermute | solution.py:10
  108.8 1.9 collective-permute-start.1
  115.2 14.4 %collective-permute-done.1 = bf16[512,256]{1,0:T(8,128)(2,1)S(1)} collective-permute-done((bf16[512,256]{1,0:T(8,128)(2,1)S(1)}, bf16[512,256]{1,0:T(8,128)(2,1)S(1)}, u32[]{:S(2)}, u32[]{:S(2)}) %collective-permute-start.1) | collective-permute-done | bytes 262176 | tf_op jit(solution)/shard_map/while/body/eval_jaxpr/ppermute | solution.py:10
  129.6 1.9 collective-permute-start.1
  136.0 14.3 %collective-permute-done.1 = bf16[512,256]{1,0:T(8,128)(2,1)S(1)} collective-permute-done((bf16[512,256]{1,0:T(8,128)(2,1)S(1)}, bf16[512,256]{1,0:T(8,128)(2,1)S(1)}, u32[]{:S(2)}, u32[]{:S(2)}) %collective-permute-start.1) | collective-permute-done | bytes 262176 | tf_op jit(solution)/shard_map/while/body/eval_jaxpr/ppermute | solution.py:10
  150.3 2.6 collective-permute-start.1
  154.8 1.4 fusion.77
  157.4 12.5 %collective-permute-done.1 = bf16[512,256]{1,0:T(8,128)(2,1)S(1)} collective-permute-done((bf16[512,256]{1,0:T(8,128)(2,1)S(1)}, bf16[512,256]{1,0:T(8,128)(2,1)S(1)}, u32[]{:S(2)}, u32[]{:S(2)}) %collective-permute-start.1) | collective-permute-done | bytes 262176 | tf_op jit(solution)/shard_map/while/body/eval_jaxpr/ppermute | solution.py:10
  169.9 3.7 collective-permute-start.1
  178.1 13.4 %collective-permute-done.1 = bf16[512,256]{1,0:T(8,128)(2,1)S(1)} collective-permute-done((bf16[512,256]{1,0:T(8,128)(2,1)S(1)}, bf16[512,256]{1,0:T(8,128)(2,1)S(1)}, u32[]{:S(2)}, u32[]{:S(2)}) %collective-permute-start.1) | collective-permute-done | bytes 262176 | tf_op jit(solution)/shard_map/while/body/eval_jaxpr/ppermute | solution.py:10
  192.1 2.6 fusion.26
  194.7 2.2 copy.14
  198.3 52.4 %reduce-scatter.3.cloned.1.call-done = f32[64,256]{1,0:T(8,128)} async-done(((f32[512,256]{1,0:T(8,128)}), f32[64,256]{1,0:T(8,128)}) %reduce-scatter.3.cloned.1.call-update) | async-done | bytes 65552 | tf_op jit(solution)/shard_map/reduce_scatter | solution.py:94
  250.7 1.5 fusion.31
  252.2 22.0 %all_gather.3 = bf16[512,256]{1,0:T(8,128)(2,1)S(1)} all-gather(bf16[64,256]{1,0:T(8,128)(2,1)S(1)} %get-tuple-element.366), channel_id=1, replica_groups=mesh['blk'=64,'rep'=8] {'rep'}, dimensions={0}, use_global_device_ids=true | all-gather | bytes 294912 | tf_op jit(solution)/shard_map/all_gather | solution.py:98
  274.2 247.6 %while.33 = (s32[]{:T(128)}, f32[512,256]{1,0:T(8,128)S(1)}, s32[8,12]{1,0:T(8,128)S(1)}, bf16[8,12,128,128]{3,2,1,0:T(8,128)(2,1)}, bf16[512,256]{1,0:T(8,128)(2,1)S(1)}, /*index=5*/s32[8]{0:T(128)S(1)}, s32[]{:T(128)}) while((s32[]{:T(128)}, f32[512,256]{1,0:T(8,128)S(1)}, s32[8,12]{1,0:T(8,128)S(1)}, bf16[8,12,128,128]{3,2,1,0:T(8,128)(2,1)}, ...), condition=%wide.region_4.5_spmd, body=%wide.region_3.4_spmd.sunk | while | flops 104334752 | bytes 11146301 | solution.py:112
  276.2 1.4 fusion.71
  278.7 6.7 collective-permute-start
  285.5 15.3 %collective-permute-done = f32[512,256]{1,0:T(8,128)S(1)} collective-permute-done((f32[512,256]{1,0:T(8,128)S(1)}, f32[512,256]{1,0:T(8,128)S(1)}, u32[]{:S(2)}, u32[]{:S(2)}) %collective-permute-start) | collective-permute-done | bytes 524320 | tf_op jit(solution)/shard_map/while/body/eval_jaxpr/ppermute | solution.py:10
  302.7 1.4 fusion.71
  305.3 1.9 collective-permute-start
  307.2 23.0 %collective-permute-done = f32[512,256]{1,0:T(8,128)S(1)} collective-permute-done((f32[512,256]{1,0:T(8,128)S(1)}, f32[512,256]{1,0:T(8,128)S(1)}, u32[]{:S(2)}, u32[]{:S(2)}) %collective-permute-start) | collective-permute-done | bytes 524320 | tf_op jit(solution)/shard_map/while/body/eval_jaxpr/ppermute | solution.py:10
  332.2 1.4 fusion.71
  334.7 1.9 collective-permute-start
  336.7 28.7 %collective-permute-done = f32[512,256]{1,0:T(8,128)S(1)} collective-permute-done((f32[512,256]{1,0:T(8,128)S(1)}, f32[512,256]{1,0:T(8,128)S(1)}, u32[]{:S(2)}, u32[]{:S(2)}) %collective-permute-start) | collective-permute-done | bytes 524320 | tf_op jit(solution)/shard_map/while/body/eval_jaxpr/ppermute | solution.py:10
  367.3 1.4 fusion.71
  369.8 1.9 collective-permute-start
  371.8 27.3 %collective-permute-done = f32[512,256]{1,0:T(8,128)S(1)} collective-permute-done((f32[512,256]{1,0:T(8,128)S(1)}, f32[512,256]{1,0:T(8,128)S(1)}, u32[]{:S(2)}, u32[]{:S(2)}) %collective-permute-start) | collective-permute-done | bytes 524320 | tf_op jit(solution)/shard_map/while/body/eval_jaxpr/ppermute | solution.py:10
  400.9 1.4 fusion.71
  403.5 1.9 collective-permute-start
  405.4 26.0 %collective-permute-done = f32[512,256]{1,0:T(8,128)S(1)} collective-permute-done((f32[512,256]{1,0:T(8,128)S(1)}, f32[512,256]{1,0:T(8,128)S(1)}, u32[]{:S(2)}, u32[]{:S(2)}) %collective-permute-start) | collective-permute-done | bytes 524320 | tf_op jit(solution)/shard_map/while/body/eval_jaxpr/ppermute | solution.py:10
  433.3 1.4 fusion.71
  435.9 1.9 collective-permute-start
  437.8 26.0 %collective-permute-done = f32[512,256]{1,0:T(8,128)S(1)} collective-permute-done((f32[512,256]{1,0:T(8,128)S(1)}, f32[512,256]{1,0:T(8,128)S(1)}, u32[]{:S(2)}, u32[]{:S(2)}) %collective-permute-start) | collective-permute-done | bytes 524320 | tf_op jit(solution)/shard_map/while/body/eval_jaxpr/ppermute | solution.py:10
  465.7 1.4 fusion.71
  468.3 1.9 collective-permute-start
  470.2 20.2 %collective-permute-done = f32[512,256]{1,0:T(8,128)S(1)} collective-permute-done((f32[512,256]{1,0:T(8,128)S(1)}, f32[512,256]{1,0:T(8,128)S(1)}, u32[]{:S(2)}, u32[]{:S(2)}) %collective-permute-start) | collective-permute-done | bytes 524320 | tf_op jit(solution)/shard_map/while/body/eval_jaxpr/ppermute | solution.py:10
  492.3 1.4 fusion.71
  494.9 1.9 collective-permute-start
  496.8 25.0 %collective-permute-done = f32[512,256]{1,0:T(8,128)S(1)} collective-permute-done((f32[512,256]{1,0:T(8,128)S(1)}, f32[512,256]{1,0:T(8,128)S(1)}, u32[]{:S(2)}, u32[]{:S(2)}) %collective-permute-start) | collective-permute-done | bytes 524320 | tf_op jit(solution)/shard_map/while/body/eval_jaxpr/ppermute | solution.py:10
  521.8 27.2 %collective-permute-start.5 = (f32[512,256]{1,0:T(8,128)S(1)}, f32[512,256]{1,0:T(8,128)S(1)}, u32[]{:S(2)}, u32[]{:S(2)}) collective-permute-start(f32[512,256]{1,0:T(8,128)S(1)} %get-tuple-element.320), channel_id=1, source_target_pairs={{8,0},{16,8},{24,16},{32,24},{40,32},{48,40},{56,48},{64,56},{72,6... | collective-permute-start | bytes 1572872 | tf_op jit(solution)/shard_map/ppermute | solution.py:10
  549.0 1.5 collective-permute-done.5
  550.6 17.8 %collective-permute-start.6 = (f32[512,256]{1,0:T(8,128)S(1)}, f32[512,256]{1,0:T(8,128)S(1)}, u32[]{:S(2)}, u32[]{:S(2)}) collective-permute-start(f32[512,256]{1,0:T(8,128)S(1)} %broadcast_select_fusion), channel_id=1, source_target_pairs={{16,0},{24,8},{32,16},{40,24},{48,32},{56,40},{64,48},{72,56},{80,... | collective-permute-start | bytes 1572872 | tf_op jit(solution)/shard_map/ppermute | solution.py:10
  568.4 70.9 %collective-permute-done.6 = f32[512,256]{1,0:T(8,128)S(1)} collective-permute-done((f32[512,256]{1,0:T(8,128)S(1)}, f32[512,256]{1,0:T(8,128)S(1)}, u32[]{:S(2)}, u32[]{:S(2)}) %collective-permute-start.6) | collective-permute-done | bytes 524320 | tf_op jit(solution)/shard_map/ppermute | solution.py:10
  639.3 3.4 collective-permute-start.7
  642.8 19.5 %collective-permute-done.7 = f32[512,256]{1,0:T(8,128)S(1)} collective-permute-done((f32[512,256]{1,0:T(8,128)S(1)}, f32[512,256]{1,0:T(8,128)S(1)}, u32[]{:S(2)}, u32[]{:S(2)}) %collective-permute-start.7) | collective-permute-done | bytes 524320 | tf_op jit(solution)/shard_map/ppermute | solution.py:10
  663.2 59.4 %reduce-scatter.5.cloned.1.call-done = f32[64,256]{1,0:T(8,128)} async-done(((f32[512,256]{1,0:T(8,128)}), f32[64,256]{1,0:T(8,128)}) %reduce-scatter.5.cloned.1.call-update) | async-done | bytes 65552 | tf_op jit(solution)/shard_map/reduce_scatter | solution.py:114
  722.7 1.7 fusion.39
  724.4 1.6 convolution_convert_fusion.1
  726.0 271.6 %all-reduce.2.cloned.1.call-done = f32[128,256]{1,0:T(8,128)} async-done(((f32[128,256]{1,0:T(8,128)}), f32[128,256]{1,0:T(8,128)}) %all-reduce.2.cloned.1.call-update) | async-done | bytes 131088 | tf_op jit(solution)/shard_map/psum | solution.py:124
  997.6 1.6 copy.43
  (181 shorter events, 60.1 us)
Async XLA Ops:
  7.2 0.9 copy-start
  7.2 44.2 %copy-start.4 = (s32[1,1,8]{2,1,0:T(1,128)S(1)}, s32[1,1,8]{2,1,0:T(1,128)}, u32[]{:S(2)}) copy-start(s32[1,1,8]{2,1,0:T(1,128)} %param.14) | copy-start | bytes 100
  7.2 31.2 %copy-start.3 = (s32[1,1,8,12]{3,2,1,0:T(8,128)S(1)}, s32[1,1,8,12]{3,2,1,0:T(8,128)}, u32[]{:S(2)}) copy-start(s32[1,1,8,12]{3,2,1,0:T(8,128)} %param.13) | copy-start | bytes 1156
  7.2 243.5 %reduce-scatter.3.cloned.1.call-start = ((), (), s32[]{:S(2)}) async-start(), calls=%async_computation.2 | async-start | bytes 589824 | tf_op jit(solution)/shard_map/reduce_scatter | solution.py:94
  9.1 9.8 collective-permute-start.2
  18.9 16.8 %collective-permute-start.3 = (bf16[512,256]{1,0:T(8,128)(2,1)S(1)}, bf16[512,256]{1,0:T(8,128)(2,1)S(1)}, u32[]{:S(2)}, u32[]{:S(2)}) collective-permute-start(bf16[512,256]{1,0:T(8,128)(2,1)S(1)} %broadcast_select_fusion.1), channel_id=1, source_target_pairs={{496,0},{504,8},{0,16},{8,24},{16,32},{24,40},{32,48},{40,56},{48,... | collective-permute-start | bytes 786440 | tf_op jit(solution)/shard_map/ppermute | solution.py:10
  35.7 15.6 %collective-permute-start.4 = (bf16[512,256]{1,0:T(8,128)(2,1)S(1)}, bf16[512,256]{1,0:T(8,128)(2,1)S(1)}, u32[]{:S(2)}, u32[]{:S(2)}) collective-permute-start(bf16[512,256]{1,0:T(8,128)(2,1)S(1)} %broadcast_select_fusion.3), channel_id=1, source_target_pairs={{480,0},{488,8},{496,16},{504,24},{0,32},{8,40},{16,48},{24,56},{3... | collective-permute-start | bytes 786440 | tf_op jit(solution)/shard_map/ppermute | solution.py:10
  51.4 16.4 %collective-permute-start.1 = (bf16[512,256]{1,0:T(8,128)(2,1)S(1)}, bf16[512,256]{1,0:T(8,128)(2,1)S(1)}, u32[]{:S(2)}, u32[]{:S(2)}) collective-permute-start(bf16[512,256]{1,0:T(8,128)(2,1)S(1)} %copy.31), channel_id=1, source_target_pairs={{448,0},{456,8},{464,16},{472,24},{480,32},{488,40},{496,48},{504,... | collective-permute-start | bytes 786440 | tf_op jit(solution)/shard_map/while/body/eval_jaxpr/ppermute | solution.py:10
  67.8 20.1 %collective-permute-start.1 = (bf16[512,256]{1,0:T(8,128)(2,1)S(1)}, bf16[512,256]{1,0:T(8,128)(2,1)S(1)}, u32[]{:S(2)}, u32[]{:S(2)}) collective-permute-start(bf16[512,256]{1,0:T(8,128)(2,1)S(1)} %copy.31), channel_id=1, source_target_pairs={{448,0},{456,8},{464,16},{472,24},{480,32},{488,40},{496,48},{504,... | collective-permute-start | bytes 786440 | tf_op jit(solution)/shard_map/while/body/eval_jaxpr/ppermute | solution.py:10
  87.9 20.9 %collective-permute-start.1 = (bf16[512,256]{1,0:T(8,128)(2,1)S(1)}, bf16[512,256]{1,0:T(8,128)(2,1)S(1)}, u32[]{:S(2)}, u32[]{:S(2)}) collective-permute-start(bf16[512,256]{1,0:T(8,128)(2,1)S(1)} %copy.31), channel_id=1, source_target_pairs={{448,0},{456,8},{464,16},{472,24},{480,32},{488,40},{496,48},{504,... | collective-permute-start | bytes 786440 | tf_op jit(solution)/shard_map/while/body/eval_jaxpr/ppermute | solution.py:10
  108.8 20.8 %collective-permute-start.1 = (bf16[512,256]{1,0:T(8,128)(2,1)S(1)}, bf16[512,256]{1,0:T(8,128)(2,1)S(1)}, u32[]{:S(2)}, u32[]{:S(2)}) collective-permute-start(bf16[512,256]{1,0:T(8,128)(2,1)S(1)} %copy.31), channel_id=1, source_target_pairs={{448,0},{456,8},{464,16},{472,24},{480,32},{488,40},{496,48},{504,... | collective-permute-start | bytes 786440 | tf_op jit(solution)/shard_map/while/body/eval_jaxpr/ppermute | solution.py:10
  129.6 20.7 %collective-permute-start.1 = (bf16[512,256]{1,0:T(8,128)(2,1)S(1)}, bf16[512,256]{1,0:T(8,128)(2,1)S(1)}, u32[]{:S(2)}, u32[]{:S(2)}) collective-permute-start(bf16[512,256]{1,0:T(8,128)(2,1)S(1)} %copy.31), channel_id=1, source_target_pairs={{448,0},{456,8},{464,16},{472,24},{480,32},{488,40},{496,48},{504,... | collective-permute-start | bytes 786440 | tf_op jit(solution)/shard_map/while/body/eval_jaxpr/ppermute | solution.py:10
  150.3 19.5 %collective-permute-start.1 = (bf16[512,256]{1,0:T(8,128)(2,1)S(1)}, bf16[512,256]{1,0:T(8,128)(2,1)S(1)}, u32[]{:S(2)}, u32[]{:S(2)}) collective-permute-start(bf16[512,256]{1,0:T(8,128)(2,1)S(1)} %copy.31), channel_id=1, source_target_pairs={{448,0},{456,8},{464,16},{472,24},{480,32},{488,40},{496,48},{504,... | collective-permute-start | bytes 786440 | tf_op jit(solution)/shard_map/while/body/eval_jaxpr/ppermute | solution.py:10
  169.9 21.6 %collective-permute-start.1 = (bf16[512,256]{1,0:T(8,128)(2,1)S(1)}, bf16[512,256]{1,0:T(8,128)(2,1)S(1)}, u32[]{:S(2)}, u32[]{:S(2)}) collective-permute-start(bf16[512,256]{1,0:T(8,128)(2,1)S(1)} %copy.31), channel_id=1, source_target_pairs={{448,0},{456,8},{464,16},{472,24},{480,32},{488,40},{496,48},{504,... | collective-permute-start | bytes 786440 | tf_op jit(solution)/shard_map/while/body/eval_jaxpr/ppermute | solution.py:10
  197.2 53.4 %copy-start.2 = (bf16[64,256]{1,0:T(8,128)(2,1)S(1)}, bf16[64,256]{1,0:T(8,128)(2,1)}, u32[]{:S(2)}) copy-start(bf16[64,256]{1,0:T(8,128)(2,1)} %param.15) | copy-start | bytes 98308
  198.3 524.4 %reduce-scatter.5.cloned.1.call-start = ((), (), s32[]{:S(2)}) async-start(), calls=%async_computation.3 | async-start | bytes 589824 | tf_op jit(solution)/shard_map/reduce_scatter | solution.py:114
  278.7 22.1 %collective-permute-start = (f32[512,256]{1,0:T(8,128)S(1)}, f32[512,256]{1,0:T(8,128)S(1)}, u32[]{:S(2)}, u32[]{:S(2)}) collective-permute-start(f32[512,256]{1,0:T(8,128)S(1)} %bitcast_add_fusion.5), channel_id=1, source_target_pairs={{448,0},{456,8},{464,16},{472,24},{480,32},{488,40},{496,48},{504,... | collective-permute-start | bytes 1572872 | tf_op jit(solution)/shard_map/while/body/eval_jaxpr/ppermute | solution.py:10
  305.3 25.0 %collective-permute-start = (f32[512,256]{1,0:T(8,128)S(1)}, f32[512,256]{1,0:T(8,128)S(1)}, u32[]{:S(2)}, u32[]{:S(2)}) collective-permute-start(f32[512,256]{1,0:T(8,128)S(1)} %bitcast_add_fusion.5), channel_id=1, source_target_pairs={{448,0},{456,8},{464,16},{472,24},{480,32},{488,40},{496,48},{504,... | collective-permute-start | bytes 1572872 | tf_op jit(solution)/shard_map/while/body/eval_jaxpr/ppermute | solution.py:10
  334.7 30.6 %collective-permute-start = (f32[512,256]{1,0:T(8,128)S(1)}, f32[512,256]{1,0:T(8,128)S(1)}, u32[]{:S(2)}, u32[]{:S(2)}) collective-permute-start(f32[512,256]{1,0:T(8,128)S(1)} %bitcast_add_fusion.5), channel_id=1, source_target_pairs={{448,0},{456,8},{464,16},{472,24},{480,32},{488,40},{496,48},{504,... | collective-permute-start | bytes 1572872 | tf_op jit(solution)/shard_map/while/body/eval_jaxpr/ppermute | solution.py:10
  369.8 29.2 %collective-permute-start = (f32[512,256]{1,0:T(8,128)S(1)}, f32[512,256]{1,0:T(8,128)S(1)}, u32[]{:S(2)}, u32[]{:S(2)}) collective-permute-start(f32[512,256]{1,0:T(8,128)S(1)} %bitcast_add_fusion.5), channel_id=1, source_target_pairs={{448,0},{456,8},{464,16},{472,24},{480,32},{488,40},{496,48},{504,... | collective-permute-start | bytes 1572872 | tf_op jit(solution)/shard_map/while/body/eval_jaxpr/ppermute | solution.py:10
  403.5 27.9 %collective-permute-start = (f32[512,256]{1,0:T(8,128)S(1)}, f32[512,256]{1,0:T(8,128)S(1)}, u32[]{:S(2)}, u32[]{:S(2)}) collective-permute-start(f32[512,256]{1,0:T(8,128)S(1)} %bitcast_add_fusion.5), channel_id=1, source_target_pairs={{448,0},{456,8},{464,16},{472,24},{480,32},{488,40},{496,48},{504,... | collective-permute-start | bytes 1572872 | tf_op jit(solution)/shard_map/while/body/eval_jaxpr/ppermute | solution.py:10
  435.9 28.0 %collective-permute-start = (f32[512,256]{1,0:T(8,128)S(1)}, f32[512,256]{1,0:T(8,128)S(1)}, u32[]{:S(2)}, u32[]{:S(2)}) collective-permute-start(f32[512,256]{1,0:T(8,128)S(1)} %bitcast_add_fusion.5), channel_id=1, source_target_pairs={{448,0},{456,8},{464,16},{472,24},{480,32},{488,40},{496,48},{504,... | collective-permute-start | bytes 1572872 | tf_op jit(solution)/shard_map/while/body/eval_jaxpr/ppermute | solution.py:10
  468.3 22.1 %collective-permute-start = (f32[512,256]{1,0:T(8,128)S(1)}, f32[512,256]{1,0:T(8,128)S(1)}, u32[]{:S(2)}, u32[]{:S(2)}) collective-permute-start(f32[512,256]{1,0:T(8,128)S(1)} %bitcast_add_fusion.5), channel_id=1, source_target_pairs={{448,0},{456,8},{464,16},{472,24},{480,32},{488,40},{496,48},{504,... | collective-permute-start | bytes 1572872 | tf_op jit(solution)/shard_map/while/body/eval_jaxpr/ppermute | solution.py:10
  494.9 27.0 %collective-permute-start = (f32[512,256]{1,0:T(8,128)S(1)}, f32[512,256]{1,0:T(8,128)S(1)}, u32[]{:S(2)}, u32[]{:S(2)}) collective-permute-start(f32[512,256]{1,0:T(8,128)S(1)} %bitcast_add_fusion.5), channel_id=1, source_target_pairs={{448,0},{456,8},{464,16},{472,24},{480,32},{488,40},{496,48},{504,... | collective-permute-start | bytes 1572872 | tf_op jit(solution)/shard_map/while/body/eval_jaxpr/ppermute | solution.py:10
  521.8 28.7 %collective-permute-start.5 = (f32[512,256]{1,0:T(8,128)S(1)}, f32[512,256]{1,0:T(8,128)S(1)}, u32[]{:S(2)}, u32[]{:S(2)}) collective-permute-start(f32[512,256]{1,0:T(8,128)S(1)} %get-tuple-element.320), channel_id=1, source_target_pairs={{8,0},{16,8},{24,16},{32,24},{40,32},{48,40},{56,48},{64,56},{72,6... | collective-permute-start | bytes 1572872 | tf_op jit(solution)/shard_map/ppermute | solution.py:10
  550.6 173.8 %copy-start.1 = (bf16[128,256]{1,0:T(8,128)(2,1)S(1)}, bf16[128,256]{1,0:T(8,128)(2,1)}, u32[]{:S(2)}) copy-start(bf16[128,256]{1,0:T(8,128)(2,1)} %param.11) | copy-start | bytes 196612
  550.6 88.7 %collective-permute-start.6 = (f32[512,256]{1,0:T(8,128)S(1)}, f32[512,256]{1,0:T(8,128)S(1)}, u32[]{:S(2)}, u32[]{:S(2)}) collective-permute-start(f32[512,256]{1,0:T(8,128)S(1)} %broadcast_select_fusion), channel_id=1, source_target_pairs={{16,0},{24,8},{32,16},{40,24},{48,32},{56,40},{64,48},{72,56},{80,... | collective-permute-start | bytes 1572872 | tf_op jit(solution)/shard_map/ppermute | solution.py:10
  639.3 22.9 %collective-permute-start.7 = (f32[512,256]{1,0:T(8,128)S(1)}, f32[512,256]{1,0:T(8,128)S(1)}, u32[]{:S(2)}, u32[]{:S(2)}) collective-permute-start(f32[512,256]{1,0:T(8,128)S(1)} %broadcast_select_fusion.2), channel_id=1, source_target_pairs={{32,0},{40,8},{48,16},{56,24},{64,32},{72,40},{80,48},{88,56},{96,... | collective-permute-start | bytes 1572872 | tf_op jit(solution)/shard_map/ppermute | solution.py:10
  663.2 334.4 %all-reduce.2.cloned.1.call-start = ((), (), s32[]{:S(2)}) async-start(), calls=%async_computation.4 | async-start | bytes 262144 | tf_op jit(solution)/shard_map/psum | solution.py:124
Sparse Core Ops, SparseCore 0:
  198.4 52.2 reduce-scatter.2
  663.3 59.3 reduce-scatter.4
  728.2 269.2 all-reduce.1
where the time goes:
time: 1010 us
  waiting for transfers between devices  791 us (78%)
  starting transfers between devices  93 us (9%)
  matrix products  42.5 us (4%)
  local copies, waits for them, and re-layouts  26.1 us (3%)
  blocking collectives  22 us (2%)
  other arithmetic  16.6 us (2%)
  between operations  14 us (1%)
    ppermute x21, waiting for transfers between devices, passed_along(): return lax.ppermute(block, axis, route)  407 us
    psum x1, waiting for transfers between devices, local(): weight_grad = lax.psum(partial_grad, ('blk', 'rep'))  272 us
    ppermute x21, starting transfers between devices, passed_along(): return lax.ppermute(block, axis, route)  92.9 us
    reduce_scatter x1, waiting for transfers between devices, local(): lax.psum_scatter(carried, 'rep', scatter_dimension=0, tiled=True)  59.4 us
    reduce_scatter x1, waiting for transfers between devices, local(): pre = lax.psum_scatter(total, 'rep', scatter_dimension=0, tiled=True)  52.4 us
    all_gather x1, blocking collectives, local(): grad_rows = lax.all_gather(pre_grad, 'rep', axis=0, tiled=True)  22 us
  transfers between devices with their start and end apart: 24, of which 24 were waited for; matrix products, arithmetic and copies ran while one was open for 3% of the time, Pallas kernels for 0%

commit v1 on v0

v1 whole, which is shorter than its diff:
```python
import jax
import jax.numpy as jnp
from jax import lax
from jax.sharding import PartitionSpec as P


def gelu_tanh(value):
    return jax.nn.gelu(value, approximate=True)


def skewed(block, sign):
    blks, reps = lax.axis_size("blk"), lax.axis_size("rep")
    route = [
        (b * reps + r, ((b + sign * r) % blks) * reps + r) for b in range(blks) for r in range(reps)
    ]
    return lax.ppermute(block, ("blk", "rep"), route)


def split_dot(left, right):
    high = left.astype(jnp.bfloat16)
    low = (left - high.astype(jnp.float32)).astype(jnp.bfloat16)
    return jnp.dot(high, right, preferred_element_type=jnp.float32) + jnp.dot(
        low, right, preferred_element_type=jnp.float32
    )


def dense_adjacency(tiles, positions, counts, group, blocks):
    sections, slots = positions.shape
    cells = jnp.arange(blocks * blocks, dtype=jnp.int32)
    live = jnp.arange(slots, dtype=jnp.int32)[None, :] < counts[:, None]
    hits = (positions[:, None, :] == cells[None, :, None]) & live[:, None, :]
    slot_of = jnp.argmax(hits, axis=-1).astype(jnp.int32)
    filled = jnp.any(hits, axis=-1)
    order = (group - jnp.arange(sections, dtype=jnp.int32)) % sections
    slot_of, filled = slot_of[order], filled[order]
    picked = tiles[order[:, None], slot_of]
    return jnp.where(filled[..., None, None], picked, jnp.zeros((), tiles.dtype)).reshape(
        sections, blocks, blocks, tiles.shape[-2], tiles.shape[-1]
    )


def local(features, weight, tile_vals, tile_pos, tile_count, cotangent):
    rep_size = lax.axis_size("rep")
    blk_size = lax.axis_size("blk")
    blk_index = lax.axis_index("blk")
    tile_size = tile_vals.shape[-1]
    rows, feat = features.shape
    blocks = rows // tile_size
    rings = [[r + k * rep_size for k in range(blk_size // rep_size)] for r in range(rep_size)]

    adjacency = dense_adjacency(
        tile_vals[0, 0], tile_pos[0, 0], tile_count[0, 0], blk_index // rep_size, blocks
    )
    gathered = lax.all_gather(skewed(features, 1), "blk", axis_index_groups=rings)
    columns = gathered.reshape(-1, blocks, tile_size, feat)
    mixed = jnp.einsum(
        "jnmik,jmkf->nif", adjacency, columns, preferred_element_type=jnp.float32
    ).reshape(rows, feat)
    mixed = lax.psum_scatter(mixed, "rep", scatter_dimension=0, tiled=True)

    pre = split_dot(mixed, weight)
    outputs, pullback = jax.vjp(gelu_tanh, pre)
    activations = outputs.astype(jnp.bfloat16)
    pre_grad = pullback(cotangent.astype(jnp.float32))[0].astype(jnp.bfloat16)
    weight_grad = lax.dot_general(
        mixed.astype(jnp.bfloat16),
        pre_grad,
        (((0,), (0,)), ((), ())),
        preferred_element_type=jnp.float32,
    )
    weight_grad = lax.psum(lax.psum(weight_grad, "rep"), "blk")
    row_grad = lax.dot_general(
        pre_grad, weight, (((1,), (1,)), ((), ())), preferred_element_type=jnp.float32
    ).astype(jnp.bfloat16)
    row_grad = lax.all_gather(row_grad, "rep", axis=0, tiled=True).reshape(blocks, tile_size, feat)
    partial = jnp.einsum(
        "jnmik,nif->jmkf", adjacency, row_grad, preferred_element_type=jnp.float32
    ).reshape(-1, rows, feat)
    partial = lax.psum_scatter(partial, "blk", scatter_dimension=0, axis_index_groups=rings)
    partial = skewed(partial, -1)
    feat_grad = lax.psum_scatter(partial, "rep", scatter_dimension=0, tiled=True)
    return (activations, feat_grad.astype(jnp.bfloat16), weight_grad)


def solution(mesh):
    placed = (
        P("blk", None),
        P(),
        P("blk", "rep", None, None, None, None),
        P("blk", "rep", None, None),
        P("blk", "rep", None),
        P(("blk", "rep"), None),
    )
    return jax.shard_map(
        local,
        mesh=mesh,
        in_specs=placed,
        out_specs=(P(("blk", "rep"), None), P(("blk", "rep"), None), P()),
        check_vma=False,
    )
```

time: 1010 us -> 916 us (0.907)
  starting transfers between devices: 93 us -> 3.63 us
  waiting for transfers between devices: 791 us -> 839 us
  matrix products: 42.5 us -> 12.8 us
    ppermute x21 -> x2, waiting for transfers between devices: 407 us -> 0.01 us  [skewed(): return lax.ppermute(block, ('blk', 'rep'), route)]
    psum x1 -> x2, waiting for transfers between devices: 272 us -> 580 us  [local(): weight_grad = lax.psum(lax.psum(weight_grad, 'rep'), 'blk')]
    ppermute x21 -> x2, starting transfers between devices: 92.9 us -> 3.39 us  [skewed(): return lax.ppermute(block, ('blk', 'rep'), route)]
    reduce_scatter x2 -> x3, waiting for transfers between devices: 112 us -> 187 us  [the longest x1 113 us: local(): lax.psum_scatter(partial, 'blk', scatter_dimension=0, axis_index_groups=r...]
    all_gather x0 -> x1, waiting for transfers between devices: none -> 72.2 us  [local(): lax.all_gather(skewed(features, 1), 'blk', axis_index_groups=rings)]
    dot_general x35 -> x6, matrix products: 42.5 us -> 12.8 us  [the longest x1 4.81 us: local(): jnp.einsum('jnmik,nif->jmkf', adjacency, row_grad, preferred_element_type...]
    convert_element_type x17 -> x1, other arithmetic: 11.9 us -> 1.36 us  [local(): return (activations, feat_grad.astype(jnp.bfloat16), weight_grad)]
  transfers between devices with their start and end apart: 24 -> 8, of which waited for: 24 -> 6; matrix products, arithmetic and copies ran while one was open for 3% -> 2% of each run, Pallas kernels for 0% -> 0%
where the time goes in v1:
time: 916 us
  waiting for transfers between devices  839 us (92%)
  blocking collectives  21.9 us (2%)
  local copies, waits for them, and re-layouts  17 us (2%)
  between operations  14.2 us (2%)
  matrix products  12.8 us (1%)
    psum x2, waiting for transfers between devices, local(): weight_grad = lax.psum(lax.psum(weight_grad, 'rep'), 'blk')  580 us
    reduce_scatter x1, waiting for transfers between devices, local(): lax.psum_scatter(partial, 'blk', scatter_dimension=0, axis_index_groups=r...  113 us
    all_gather x1, waiting for transfers between devices, local(): lax.all_gather(skewed(features, 1), 'blk', axis_index_groups=rings)  72.2 us
    reduce_scatter x1, waiting for transfers between devices, local(): lax.psum_scatter(partial, 'rep', scatter_dimension=0, tiled=True)  45.1 us
    reduce_scatter x1, waiting for transfers between devices, local(): mixed = lax.psum_scatter(mixed, 'rep', scatter_dimension=0, tiled=True)  29.8 us
    all_gather x1, blocking collectives, local(): lax.all_gather(row_grad, 'rep', axis=0, tiled=True)  21.9 us
  transfers between devices with their start and end apart: 8, of which 6 were waited for; matrix products, arithmetic and copies ran while one was open for 2% of the time, Pallas kernels for 0%

profile of v1, /device:TPU:1, one launch (start us, length us, event | category | flops | bytes accessed | tf_op | source)
XLA Modules:
  0.0 915.5 jit_solution(509710526468673986)
XLA Ops:
  7.2 0.0 copy-start
  7.2 0.0 all-gather.3.cloned.1.call-start
  7.2 1.8 collective-permute-start
  9.0 0.0 collective-permute-done
  9.0 0.0 copy-start.3
  9.0 0.7 copy-done.3
  9.7 0.0 all-gather.3.cloned.1.call-update
  9.7 0.0 reduce-scatter.4.cloned.1.call-start
  9.8 0.8 copy.13
  10.6 0.7 iota_compare_fusion.1
  11.2 0.7 iota_reduce_fusion
  11.9 0.6 gather_fusion.1
  12.5 0.1 fusion.16
  12.5 0.1 reshape.130
  12.6 0.1 fusion.13
  12.7 0.6 gather_fusion
  13.3 0.1 copy.14
  13.4 0.1 copy.15
  13.5 0.0 copy-done
  13.5 3.1 gather_fusion.2
  16.6 3.9 fusion
  20.5 2.3 copy.16
  22.7 72.2 %all-gather.3.cloned.1.call-done = bf16[4096,128]{1,0:T(8,128)(2,1)} async-done(((bf16[512,128]{1,0:T(8,128)(2,1)}), bf16[4096,128]{1,0:T(8,128)(2,1)}) %all-gather.3.cloned.1.call-update) | async-done | bytes 1048592 | tf_op jit(solution)/shard_map/all_gather | solution.py:54
  94.9 4.4 convolution_bitcast_fusion.1
  99.4 0.0 reduce-scatter.4.cloned.1.call-update
  99.4 0.0 reduce-scatter.6.cloned.1.call-start
  99.4 0.0 copy-start.1
  99.4 0.0 copy-start.5
  99.5 6.5 copy.17
  105.9 29.8 %reduce-scatter.4.cloned.1.call-done = f32[64,128]{1,0:T(8,128)} async-done(((f32[512,128]{1,0:T(8,128)}), f32[64,128]{1,0:T(8,128)}) %reduce-scatter.4.cloned.1.call-update) | async-done | bytes 32784 | tf_op jit(solution)/shard_map/reduce_scatter | solution.py:59
  135.7 0.0 copy-done.1
  135.7 0.9 fusion.25
  136.6 0.0 copy-done.5
  136.6 1.6 fusion.4
  138.3 0.1 convolution_convert_fusion
  138.4 21.9 %all_gather.11 = bf16[512,128]{1,0:T(8,128)(2,1)S(1)} all-gather(bf16[64,128]{1,0:T(8,128)(2,1)S(1)} %convolution_convert_fusion), channel_id=1, replica_groups=mesh['blk'=64,'rep'=8] {'rep'}, dimensions={0}, use_global_device_ids=true | all-gather | bytes 147456 | tf_op jit(solution)/shard_map/all_gather | solution.py:75
  160.3 0.0 copy-start.4
  160.3 4.8 convolution_bitcast_fusion
  165.1 0.0 reduce-scatter.6.cloned.1.call-update
  165.2 0.0 all-reduce.3.cloned.1.call-start
  165.2 112.6 %reduce-scatter.6.cloned.1.call-done = f32[1,512,128]{2,1,0:T(8,128)} async-done(((f32[8,512,128]{2,1,0:T(8,128)}), f32[1,512,128]{2,1,0:T(8,128)}) %reduce-scatter.6.cloned.1.call-update) | async-done | bytes 262160 | tf_op jit(solution)/shard_map/reduce_scatter | solution.py:79
  277.8 1.6 collective-permute-start.1
  279.4 0.0 copy-done.4
  279.4 0.9 fusion.22
  280.2 0.0 all-reduce.3.cloned.1.call-update
  280.2 0.0 reduce-scatter.8.cloned.1.call-start
  280.3 0.0 collective-permute-done.1
  280.3 0.0 copy-start.2
  280.3 0.7 copy-done.2
  281.0 0.0 reduce-scatter.8.cloned.1.call-update
  281.0 0.0 all-reduce.5.cloned.1.call-start
  281.1 80.8 %all-reduce.3.cloned.1.call-done = f32[128,256]{1,0:T(8,128)} async-done(((f32[128,256]{1,0:T(8,128)}), f32[128,256]{1,0:T(8,128)}) %all-reduce.3.cloned.1.call-update) | async-done | bytes 131088 | tf_op jit(solution)/shard_map/psum | solution.py:71
  361.9 0.0 all-reduce.5.cloned.1.call-update
  361.9 45.1 %reduce-scatter.8.cloned.1.call-done = f32[64,128]{1,0:T(8,128)} async-done(((f32[512,128]{1,0:T(8,128)}), f32[64,128]{1,0:T(8,128)}) %reduce-scatter.8.cloned.1.call-update) | async-done | bytes 32784 | tf_op jit(solution)/shard_map/reduce_scatter | solution.py:81
  407.0 1.4 convert_element_type.32
  408.4 498.8 %all-reduce.5.cloned.1.call-done = f32[128,256]{1,0:T(8,128)} async-done(((f32[128,256]{1,0:T(8,128)}), f32[128,256]{1,0:T(8,128)}) %all-reduce.5.cloned.1.call-update) | async-done | bytes 131088 | tf_op jit(solution)/shard_map/psum | solution.py:71
  907.1 1.6 copy.22
  (3 shorter events, 0.0 us)
Async XLA Ops:
  7.2 6.3 copy-start
  7.2 87.7 %all-gather.3.cloned.1.call-start = ((), (), s32[]{:S(2)}) async-start(), calls=%async_computation.8 | async-start | bytes 1179648 | tf_op jit(solution)/shard_map/all_gather | solution.py:54
  7.2 1.8 collective-permute-start
  9.0 0.7 copy-start.3
  9.7 126.0 %reduce-scatter.4.cloned.1.call-start = ((), (), s32[]{:S(2)}) async-start(), calls=%async_computation.3 | async-start | bytes 294912 | tf_op jit(solution)/shard_map/reduce_scatter | solution.py:59
  99.4 178.4 %reduce-scatter.6.cloned.1.call-start = ((), (), s32[]{:S(2)}) async-start(), calls=%async_computation.4 | async-start | bytes 2359296 | tf_op jit(solution)/shard_map/reduce_scatter | solution.py:79
  99.4 36.3 %copy-start.1 = (bf16[128,256]{1,0:T(8,128)(2,1)S(1)}, bf16[128,256]{1,0:T(8,128)(2,1)}, u32[]{:S(2)}) copy-start(bf16[128,256]{1,0:T(8,128)(2,1)} %param.7) | copy-start | bytes 196612
  99.4 37.2 %copy-start.5 = (bf16[64,256]{1,0:T(8,128)(2,1)S(1)}, bf16[64,256]{1,0:T(8,128)(2,1)}, u32[]{:S(2)}) copy-start(bf16[64,256]{1,0:T(8,128)(2,1)} %param.11) | copy-start | bytes 98308
  160.3 119.0 %copy-start.4 = (f32[64,128]{1,0:T(8,128)S(1)}, f32[64,128]{1,0:T(8,128)}, u32[]{:S(2)}) copy-start(f32[64,128]{1,0:T(8,128)} %reduce-scatter.4.cloned.1.call-done) | copy-start | bytes 98308
  165.2 196.7 %all-reduce.3.cloned.1.call-start = ((), (), s32[]{:S(2)}) async-start(), calls=%async_computation.6 | async-start | bytes 262144 | tf_op jit(solution)/shard_map/psum | solution.py:71
  277.8 2.5 collective-permute-start.1
  280.2 126.8 %reduce-scatter.8.cloned.1.call-start = ((), (), s32[]{:S(2)}) async-start(), calls=%async_computation.5 | async-start | bytes 294912 | tf_op jit(solution)/shard_map/reduce_scatter | solution.py:81
  280.3 0.7 copy-start.2
  281.0 626.1 %all-reduce.5.cloned.1.call-start = ((), (), s32[]{:S(2)}) async-start(), calls=%async_computation.7 | async-start | bytes 262144 | tf_op jit(solution)/shard_map/psum | solution.py:71
Sparse Core Ops, SparseCore 0:
  11.8 83.0 all-gather.2
  99.5 36.1 reduce-scatter.3
  165.3 112.4 reduce-scatter.5
  281.1 80.7 all-reduce.2
  364.5 42.4 reduce-scatter.7
  409.8 497.3 all-reduce.4

commit v2 on v1

v2 whole, which is shorter than its diff:
```python
import functools
import math

import jax
import jax.numpy as jnp
from jax import lax
from jax.experimental import pallas as pl
from jax.experimental.pallas import tpu as pltpu
from jax.sharding import PartitionSpec as P

MESH = pl.DeviceIdType.MESH


def place_kernel(blocks, pos_ref, count_ref, tiles_ref, out_ref):
    section = pl.program_id(0)
    tile = tiles_ref.shape[-1]
    out_ref[...] = jnp.zeros_like(out_ref)
    for slot in range(tiles_ref.shape[1]):

        @pl.when(slot < count_ref[section])
        def _():
            position = pos_ref[section, slot]
            row = pl.multiple_of(lax.div(position, blocks) * tile, tile)
            column = pl.multiple_of(lax.rem(position, blocks) * tile, tile)
            out_ref[0, pl.ds(row, tile), pl.ds(column, tile)] = tiles_ref[0, slot]


def dense_adjacency(tiles, positions, counts, blocks):
    sections, slots, tile, _ = tiles.shape
    side = blocks * tile
    return pl.pallas_call(
        functools.partial(place_kernel, blocks),
        grid_spec=pltpu.PrefetchScalarGridSpec(
            num_scalar_prefetch=2,
            grid=(sections,),
            in_specs=[pl.BlockSpec((1, slots, tile, tile), lambda j, p, c: (j, 0, 0, 0))],
            out_specs=pl.BlockSpec((1, side, side), lambda j, p, c: (j, 0, 0)),
        ),
        out_shape=jax.ShapeDtypeStruct((sections, side, side), tiles.dtype),
    )(positions, counts, tiles)


def gelu_and_slope(value):
    scale = math.sqrt(2.0 / math.pi)
    square = value * value
    bend = jnp.tanh(scale * (value + 0.044715 * (square * value)))
    half = 0.5 * (1.0 + bend)
    slope = half + 0.5 * value * (1.0 - bend * bend) * (
        scale * (1.0 + 3.0 * 0.044715 * square)
    )
    return value * half, slope


def dot(left, right, contract=(1, 0)):
    return lax.dot_general(
        left,
        right,
        (((contract[0],), (contract[1],)), ((), ())),
        preferred_element_type=jnp.float32,
    )


def layer_kernel(
    blks,
    reps,
    features_ref,
    weight_ref,
    adj_ref,
    cot_ref,
    act_ref,
    feat_ref,
    wgrad_ref,
    xs,
    total,
    ysend,
    yrecv,
    urows,
    psend,
    precv,
    hsend,
    hrecv,
    wsend,
    wrecv,
    ring_out,
    ring_in,
    low_out,
    low_in,
    wall,
    x_ss,
    x_rs,
    y_ss,
    y_rs,
    u_ss,
    u_rs,
    p_ss,
    p_rs,
    h_ss,
    h_rs,
    w_ss,
    w_rs,
    ring_ss,
    ring_rs,
    low_ss,
    low_rs,
    g_ss,
    g_rs,
):
    b = lax.axis_index("blk")
    r = lax.axis_index("rep")
    sections = blks // reps
    share = cot_ref.shape[0]
    rows = features_ref.shape[0]
    wshare = wsend.shape[1]

    def ahead(j):
        return (lax.rem(b + r + reps * j, blks), r)

    def behind(j):
        return (lax.rem(b - r - reps * j + 2 * blks, blks), r)

    def rep_peer(i):
        return (b, lax.rem(r + i, reps))

    def ring_peer(i):
        return (lax.rem(b + reps * i, blks), r)

    def low_peer(i):
        low = lax.rem(b, reps)
        return (b - low + lax.rem(low + i, reps), r)

    def remote(src, dst, ss, rs, device):
        return pltpu.make_async_remote_copy(
            src_ref=src,
            dst_ref=dst,
            send_sem=ss,
            recv_sem=rs,
            device_id=device,
            device_id_type=MESH,
        )

    barrier = pltpu.get_barrier_semaphore()

    def greet(device):
        pl.semaphore_signal(barrier, inc=1, device_id=device, device_id_type=MESH)

    @pl.when(r != 0)
    def _():
        greet(ahead(0))
        greet(behind(0))

    for j in range(1, sections):
        greet(ahead(j))
        greet(behind(j))
        greet(ring_peer(j))
    for i in range(1, reps):
        greet(rep_peer(i))
        greet(low_peer(i))
    greeted = 3 * (sections - 1) + 2 * (reps - 1)
    pl.semaphore_wait(barrier, jnp.where(r == 0, greeted, greeted + 2))

    def x_copy(j):
        return remote(features_ref, xs.at[j], x_ss.at[j], x_rs.at[j], ahead(j))

    own_x = pltpu.make_async_copy(features_ref, xs.at[0], x_rs.at[0])

    @pl.when(r != 0)
    def _():
        x_copy(0).start()

    @pl.when(r == 0)
    def _():
        own_x.start()

    for j in range(1, sections):
        x_copy(j).start()

    @pl.when(r != 0)
    def _():
        x_copy(0).wait_recv()

    @pl.when(r == 0)
    def _():
        own_x.wait()

    total[...] = dot(adj_ref[0], xs[0])

    def forward(j, carry):
        x_copy(j).wait_recv()
        total[...] += dot(adj_ref[j], xs[j])
        return carry

    lax.fori_loop(1, sections, forward, 0)

    ysend[...] = total[...].reshape(reps, share, total.shape[1])

    def to_peers(copy, count):
        for i in range(1, count):
            copy(i).start()

    def take(copy, count):
        for i in range(1, count):
            copy(i).wait_recv()

    def y_copy(i):
        peer = rep_peer(i)
        return remote(ysend.at[peer[1]], yrecv.at[i], y_ss.at[i], y_rs.at[i], peer)

    to_peers(y_copy, reps)
    mixed = ysend[r]
    for i in range(1, reps):
        y_copy(i).wait_recv()
        mixed = mixed + yrecv[i]

    weight = weight_ref[...]
    high = mixed.astype(jnp.bfloat16)
    low = (mixed - high.astype(jnp.float32)).astype(jnp.bfloat16)
    act, slope = gelu_and_slope(dot(high, weight) + dot(low, weight))
    act_ref[...] = act.astype(jnp.bfloat16)
    pre_grad = (cot_ref[...].astype(jnp.float32) * slope).astype(jnp.bfloat16)
    urows[r] = dot(pre_grad, weight, (1, 1)).astype(jnp.bfloat16)

    def u_copy(i):
        return remote(urows.at[r], urows.at[r], u_ss.at[i], u_rs.at[i], rep_peer(i))

    def u_arrival(i):
        source = lax.rem(r - i + reps, reps)
        return remote(urows.at[source], urows.at[source], u_ss.at[i], u_rs.at[i], rep_peer(i))

    to_peers(u_copy, reps)
    wsend[...] = dot(high, pre_grad, (0, 0)).reshape(wsend.shape)

    def w_copy(i):
        peer = rep_peer(i)
        return remote(wsend.at[peer[1]], wrecv.at[i], w_ss.at[i], w_rs.at[i], peer)

    to_peers(w_copy, reps)
    take(u_arrival, reps)
    flipped = urows[...].reshape(rows, urows.shape[2]).T

    def p_copy(j):
        return remote(psend.at[j], precv.at[j], p_ss.at[j], p_rs.at[j], behind(j))

    own_p = pltpu.make_async_copy(psend.at[0], precv.at[0], p_rs.at[0])
    psend[0] = dot(flipped, adj_ref[0]).astype(jnp.bfloat16)

    @pl.when(r != 0)
    def _():
        p_copy(0).start()

    @pl.when(r == 0)
    def _():
        own_p.start()

    def backward(j, carry):
        psend[j] = dot(flipped, adj_ref[j]).astype(jnp.bfloat16)
        p_copy(j).start()
        return carry

    lax.fori_loop(1, sections, backward, 0)

    part = wsend[r]
    for i in range(1, reps):
        w_copy(i).wait_recv()
        part = part + wrecv[i]
    ring_out[...] = part

    def ring_copy(i):
        return remote(ring_out, ring_in.at[i], ring_ss.at[i], ring_rs.at[i], ring_peer(i))

    to_peers(ring_copy, sections)
    for i in range(1, sections):
        ring_copy(i).wait_recv()
        part = part + ring_in[i]
    low_out[...] = part

    def low_copy(i):
        return remote(low_out, low_in.at[i], low_ss.at[i], low_rs.at[i], low_peer(i))

    to_peers(low_copy, reps)

    @pl.when(r != 0)
    def _():
        p_copy(0).wait_recv()

    @pl.when(r == 0)
    def _():
        own_p.wait()

    def gather(j, summed):
        p_copy(j).wait_recv()
        return summed + precv[j].astype(jnp.float32)

    summed = precv[0].astype(jnp.float32)
    for j in range(1, sections):
        summed = gather(j, summed)
    hsend[...] = summed.T.reshape(hsend.shape)

    def h_copy(i):
        peer = rep_peer(i)
        return remote(hsend.at[peer[1]], hrecv.at[i], h_ss.at[i], h_rs.at[i], peer)

    to_peers(h_copy, reps)
    part = low_out[...]
    for i in range(1, reps):
        low_copy(i).wait_recv()
        part = part + low_in[i]
    wall[r] = part

    def g_copy(i):
        return remote(wall.at[r], wall.at[r], g_ss.at[i], g_rs.at[i], rep_peer(i))

    def g_arrival(i):
        source = lax.rem(r - i + reps, reps)
        return remote(wall.at[source], wall.at[source], g_ss.at[i], g_rs.at[i], rep_peer(i))

    to_peers(g_copy, reps)
    rows_grad = hsend[r]
    for i in range(1, reps):
        h_copy(i).wait_recv()
        rows_grad = rows_grad + hrecv[i]
    feat_ref[...] = rows_grad.astype(jnp.bfloat16)
    take(g_arrival, reps)
    wgrad_ref[...] = wall[...].reshape(wgrad_ref.shape)

    @pl.when(r != 0)
    def _():
        x_copy(0).wait_send()
        p_copy(0).wait_send()

    for j in range(1, sections):
        x_copy(j).wait_send()
        p_copy(j).wait_send()
        ring_copy(j).wait_send()
    for i in range(1, reps):
        y_copy(i).wait_send()
        u_copy(i).wait_send()
        w_copy(i).wait_send()
        h_copy(i).wait_send()
        low_copy(i).wait_send()
        g_copy(i).wait_send()


def local(features, weight, tile_vals, tile_pos, tile_count, cotangent):
    reps = lax.axis_size("rep")
    blks = lax.axis_size("blk")
    sections = blks // reps
    rows, feat = features.shape
    hid = weight.shape[1]
    share = rows // reps
    wshare = feat // reps
    adjacency = dense_adjacency(
        tile_vals[0, 0], tile_pos[0, 0], tile_count[0, 0], rows // tile_vals.shape[-1]
    )
    bf, fl = jnp.bfloat16, jnp.float32
    sems = [sections] * 2 + [reps] * 4 + [sections] * 2 + [reps] * 4 + [sections] * 2 + [reps] * 4
    act, feat_grad, weight_grad = pl.pallas_call(
        functools.partial(layer_kernel, blks, reps),
        out_shape=(
            jax.ShapeDtypeStruct((share, hid), bf),
            jax.ShapeDtypeStruct((share, feat), bf),
            jax.ShapeDtypeStruct((feat, hid), fl),
        ),
        in_specs=[pl.BlockSpec(memory_space=pltpu.VMEM)] * 4,
        out_specs=[pl.BlockSpec(memory_space=pltpu.VMEM)] * 3,
        scratch_shapes=[
            pltpu.VMEM((sections, rows, feat), bf),
            pltpu.VMEM((rows, feat), fl),
            pltpu.VMEM((reps, share, feat), fl),
            pltpu.VMEM((reps, share, feat), fl),
            pltpu.VMEM((reps, share, feat), bf),
            pltpu.VMEM((sections, feat, rows), bf),
            pltpu.VMEM((sections, feat, rows), bf),
            pltpu.VMEM((reps, share, feat), fl),
            pltpu.VMEM((reps, share, feat), fl),
            pltpu.VMEM((reps, wshare, hid), fl),
            pltpu.VMEM((reps, wshare, hid), fl),
            pltpu.VMEM((wshare, hid), fl),
            pltpu.VMEM((sections, wshare, hid), fl),
            pltpu.VMEM((wshare, hid), fl),
            pltpu.VMEM((reps, wshare, hid), fl),
            pltpu.VMEM((reps, wshare, hid), fl),
        ]
        + [pltpu.SemaphoreType.DMA((n,)) for n in sems],
        compiler_params=pltpu.CompilerParams(
            collective_id=0, has_side_effects=True, vmem_limit_bytes=48 << 20
        ),
    )(features, weight, adjacency, cotangent)
    return (act, feat_grad, weight_grad)


def solution(mesh):
    placed = (
        P("blk", None),
        P(),
        P("blk", "rep", None, None, None, None),
        P("blk", "rep", None, None),
        P("blk", "rep", None),
        P(("blk", "rep"), None),
    )
    return jax.shard_map(
        local,
        mesh=mesh,
        in_specs=placed,
        out_specs=(P(("blk", "rep"), None), P(("blk", "rep"), None), P()),
        check_vma=False,
    )
```

time: 916 us -> 146 us (0.16)
  the two profiles are of different devices: /device:TPU:1 before, /device:TPU:56 now
where the time goes in v2:
time: 146 us
  Pallas kernels  141 us (97%)
  local copies, waits for them, and re-layouts  4.07 us (3%)
    pallas_call x1, Pallas kernels, local(): pl.pallas_call(functools.partial(layer_kernel, blks, reps), out_shape=(ja...  133 us
    pallas_call x1, Pallas kernels, dense_adjacency(): pl.pallas_call(functools.partial(place_kernel, blocks), grid_spec=pltpu.P...  7.75 us
    unnamed x11, local copies, waits for them, and re-layouts  4.07 us

profile of v2, /device:TPU:56, one launch (start us, length us, event | category | flops | bytes accessed | tf_op | source)
XLA Modules:
  0.0 145.8 jit_solution(13346764048547210831)
XLA Ops:
  0.6 0.0 copy-start.3
  0.6 0.0 copy-start.2
  0.7 0.0 copy-start.1
  0.7 7.7 %shard_map.85.adj_ref = bf16[8,512,512]{2,1,0:T(8,128)(2,1)} custom-call(s32[8,12]{1,0:T(8,128)} %bitcast.4, s32[8]{0:T(128)} %bitcast.5, bf16[8,12,128,128]{3,2,1,0:T(8,128)(2,1)} %bitcast.3), custom_call_target="tpu_custom_call" | custom-call | tf_op jit(solution)/shard_map/pallas_call | solution.py:31
  8.4 0.0 copy-done.3
  8.4 0.0 copy-done.2
  8.4 0.0 copy-done.1
  8.4 0.0 copy-start
  8.4 2.2 %copy-done = bf16[8,512,512]{2,1,0:T(8,128)(2,1)S(1)} copy-done((bf16[8,512,512]{2,1,0:T(8,128)(2,1)S(1)}, bf16[8,512,512]{2,1,0:T(8,128)(2,1)}, u32[]{:S(2)}) %copy-start) | copy-done | bytes 4194328
  10.6 133.3 %shard_map.86 = (bf16[64,256]{1,0:T(8,128)(2,1)S(1)}, bf16[64,128]{1,0:T(8,128)(2,1)S(1)}, f32[128,256]{1,0:T(8,128)S(1)}) custom-call(bf16[512,128]{1,0:T(8,128)(2,1)S(1)} %copy-done.1, bf16[128,256]{1,0:T(8,128)(2,1)S(1)} %copy-done.2, bf16[8,512,512]{2,1,0:T(8,128)(2,1)S(1)} %copy-done, bf16[64,256]{1,0:T(8,128)(2,1)S(1)} %copy-done.3), custom_call_target="tpu_custom_call" | custom-call | tf_op jit(solution)/shard_map/pallas_call | solution.py:356
  144.0 0.6 copy.12
  144.6 0.6 copy.13
  145.2 0.7 copy.14
Async XLA Ops:
  0.6 7.8 %copy-start.3 = (bf16[64,256]{1,0:T(8,128)(2,1)S(1)}, bf16[64,256]{1,0:T(8,128)(2,1)}, u32[]{:S(2)}) copy-start(bf16[64,256]{1,0:T(8,128)(2,1)} %cot_ref.1) | copy-start | bytes 98308
  0.6 7.8 %copy-start.2 = (bf16[128,256]{1,0:T(8,128)(2,1)S(1)}, bf16[128,256]{1,0:T(8,128)(2,1)}, u32[]{:S(2)}) copy-start(bf16[128,256]{1,0:T(8,128)(2,1)} %weight_ref.1) | copy-start | bytes 196612
  0.7 7.8 %copy-start.1 = (bf16[512,128]{1,0:T(8,128)(2,1)S(1)}, bf16[512,128]{1,0:T(8,128)(2,1)}, u32[]{:S(2)}) copy-start(bf16[512,128]{1,0:T(8,128)(2,1)} %features_ref.1) | copy-start | bytes 393220
  8.4 2.2 %copy-start = (bf16[8,512,512]{2,1,0:T(8,128)(2,1)S(1)}, bf16[8,512,512]{2,1,0:T(8,128)(2,1)}, u32[]{:S(2)}) copy-start(bf16[8,512,512]{2,1,0:T(8,128)(2,1)} %shard_map.85.adj_ref) | copy-start | bytes 12582916

commit v3 on v2

--- a/solution.py
+++ b/solution.py
@@ -11,33 +11,11 @@
 MESH = pl.DeviceIdType.MESH
 
 
-def place_kernel(blocks, pos_ref, count_ref, tiles_ref, out_ref):
-    section = pl.program_id(0)
-    tile = tiles_ref.shape[-1]
-    out_ref[...] = jnp.zeros_like(out_ref)
-    for slot in range(tiles_ref.shape[1]):
-
-        @pl.when(slot < count_ref[section])
-        def _():
-            position = pos_ref[section, slot]
-            row = pl.multiple_of(lax.div(position, blocks) * tile, tile)
-            column = pl.multiple_of(lax.rem(position, blocks) * tile, tile)
-            out_ref[0, pl.ds(row, tile), pl.ds(column, tile)] = tiles_ref[0, slot]
-
-
-def dense_adjacency(tiles, positions, counts, blocks):
-    sections, slots, tile, _ = tiles.shape
-    side = blocks * tile
-    return pl.pallas_call(
-        functools.partial(place_kernel, blocks),
-        grid_spec=pltpu.PrefetchScalarGridSpec(
-            num_scalar_prefetch=2,
-            grid=(sections,),
-            in_specs=[pl.BlockSpec((1, slots, tile, tile), lambda j, p, c: (j, 0, 0, 0))],
-            out_specs=pl.BlockSpec((1, side, side), lambda j, p, c: (j, 0, 0)),
-        ),
-        out_shape=jax.ShapeDtypeStruct((sections, side, side), tiles.dtype),
-    )(positions, counts, tiles)
+def slot_codes(positions, counts, cells):
+    slots = jnp.arange(positions.shape[1], dtype=jnp.int32)[None, None, :]
+    hits = positions[:, None, :] == jnp.arange(cells, dtype=jnp.int32)[None, :, None]
+    hits = hits & (slots < counts[:, None, None])
+    return jnp.sum(jnp.where(hits, slots + 1, 0), axis=-1, dtype=jnp.int32)
 
 
 def gelu_and_slope(value):
@@ -65,16 +43,19 @@
     reps,
     features_ref,
     weight_ref,
-    adj_ref,
+    tiles_ref,
+    code_ref,
     cot_ref,
     act_ref,
     feat_ref,
     wgrad_ref,
+    adj_ref,
     xs,
     total,
     ysend,
     yrecv,
     urows,
+    kept,
     psend,
     precv,
     hsend,
@@ -110,13 +91,24 @@
     sections = blks // reps
     share = cot_ref.shape[0]
     rows = features_ref.shape[0]
-    wshare = wsend.shape[1]
-
-    def ahead(j):
-        return (lax.rem(b + r + reps * j, blks), r)
-
-    def behind(j):
-        return (lax.rem(b - r - reps * j + 2 * blks, blks), r)
+
+    span = 2 * reps
+    turns = sections // 2
+    z = lax.div(b, span)
+    q = lax.rem(b, span)
+
+    def ahead(s):
+        return (z * span + lax.rem(q + r + reps * s, span), r)
+
+    def behind(s):
+        return (z * span + lax.rem(q - r - reps * s + 2 * span, span), r)
+
+    up = (lax.rem(z + 1, turns) * span + q, r)
+    down = (lax.rem(z + turns - 1, turns) * span + q, r)
+
+    def section_of(g, s):
+        wrapped = (q - r - reps * s < 0).astype(jnp.int32)
+        return lax.rem(2 * (g - wrapped) + s + sections, sections)
 
     def rep_peer(i):
         return (b, lax.rem(r + i, reps))
@@ -148,48 +140,85 @@
         greet(ahead(0))
         greet(behind(0))
 
+    greet(ahead(1))
+    greet(behind(1))
+    greet(up)
+    greet(down)
     for j in range(1, sections):
-        greet(ahead(j))
-        greet(behind(j))
         greet(ring_peer(j))
     for i in range(1, reps):
         greet(rep_peer(i))
         greet(low_peer(i))
-    greeted = 3 * (sections - 1) + 2 * (reps - 1)
+    greeted = 4 + (sections - 1) + 2 * (reps - 1)
     pl.semaphore_wait(barrier, jnp.where(r == 0, greeted, greeted + 2))
 
-    def x_copy(j):
-        return remote(features_ref, xs.at[j], x_ss.at[j], x_rs.at[j], ahead(j))
+    def x_copy(g, s):
+        at = 2 * g + s
+        if g == 0:
+            source, device = features_ref, ahead(s)
+        elif g == 1:
+            source, device = xs.at[s], up
+        elif g == 3:
+            source, device = xs.at[s], down
+        else:
+            source, device = xs.at[2 if s == 0 else 7], (up if s == 0 else down)
+        return remote(source, xs.at[at], x_ss.at[at], x_rs.at[at], device)
 
     own_x = pltpu.make_async_copy(features_ref, xs.at[0], x_rs.at[0])
 
     @pl.when(r != 0)
     def _():
-        x_copy(0).start()
+        x_copy(0, 0).start()
 
     @pl.when(r == 0)
     def _():
         own_x.start()
 
-    for j in range(1, sections):
-        x_copy(j).start()
-
-    @pl.when(r != 0)
-    def _():
-        x_copy(0).wait_recv()
+    x_copy(0, 1).start()
+
+    tile = tiles_ref.shape[-1]
+    blocks = rows // tile
+
+    def place(j, carry):
+        for n in range(blocks):
+            for m in range(blocks):
+                code = code_ref[j, n * blocks + m]
+                picked = tiles_ref[j, jnp.maximum(code - 1, 0)]
+                adj_ref[j, n * tile : (n + 1) * tile, m * tile : (m + 1) * tile] = jnp.where(
+                    code > 0, picked, jnp.zeros_like(picked)
+                )
+        return carry
+
+    lax.fori_loop(0, sections, place, 0)
+
+    @pl.when(r != 0)
+    def _():
+        x_copy(0, 0).wait_recv()
 
     @pl.when(r == 0)
     def _():
         own_x.wait()
 
-    total[...] = dot(adj_ref[0], xs[0])
-
-    def forward(j, carry):
-        x_copy(j).wait_recv()
-        total[...] += dot(adj_ref[j], xs[j])
-        return carry
-
-    lax.fori_loop(1, sections, forward, 0)
+    x_copy(1, 0).start()
+    x_copy(3, 0).start()
+
+    def term(g, s):
+        return dot(adj_ref[section_of(g, s)], xs[2 * g + s])
+
+    total[...] = term(0, 0)
+    x_copy(0, 1).wait_recv()
+    x_copy(3, 1).start()
+    x_copy(1, 1).start()
+    total[...] += term(0, 1)
+    x_copy(1, 0).wait_recv()
+    x_copy(2, 0).start()
+    total[...] += term(1, 0)
+    x_copy(3, 1).wait_recv()
+    x_copy(2, 1).start()
+    total[...] += term(3, 1)
+    for g, s in ((3, 0), (1, 1), (2, 0), (2, 1)):
+        x_copy(g, s).wait_recv()
+        total[...] += term(g, s)
 
     ysend[...] = total[...].reshape(reps, share, total.shape[1])
 
@@ -237,26 +266,25 @@
     take(u_arrival, reps)
     flipped = urows[...].reshape(rows, urows.shape[2]).T
 
-    def p_copy(j):
-        return remote(psend.at[j], precv.at[j], p_ss.at[j], p_rs.at[j], behind(j))
-
-    own_p = pltpu.make_async_copy(psend.at[0], precv.at[0], p_rs.at[0])
-    psend[0] = dot(flipped, adj_ref[0]).astype(jnp.bfloat16)
-
-    @pl.when(r != 0)
-    def _():
-        p_copy(0).start()
-
-    @pl.when(r == 0)
-    def _():
-        own_p.start()
-
-    def backward(j, carry):
-        psend[j] = dot(flipped, adj_ref[j]).astype(jnp.bfloat16)
-        p_copy(j).start()
-        return carry
-
-    lax.fori_loop(1, sections, backward, 0)
+    def p_copy(at):
+        device = (down, up, down, down, up, up, behind(0), behind(1))[at]
+        return remote(psend.at[at], precv.at[at], p_ss.at[at], p_rs.at[at], device)
+
+    own_p = pltpu.make_async_copy(psend.at[6], precv.at[6], p_rs.at[6])
+
+    def back(g, s):
+        return dot(flipped, adj_ref[section_of(g, s)])
+
+    for at, g, s in ((0, 2, 0), (1, 2, 1), (3, 1, 1), (4, 3, 0)):
+        psend[at] = back(g, s).astype(jnp.bfloat16)
+        p_copy(at).start()
+    kept[0] = back(0, 0)
+    kept[1] = back(0, 1)
+    for near, at, g, s in ((0, 2, 1, 0), (1, 5, 3, 1)):
+        mine = back(g, s)
+        p_copy(near).wait_recv()
+        psend[at] = (mine + precv[near].astype(jnp.float32)).astype(jnp.bfloat16)
+        p_copy(at).start()
 
     part = wsend[r]
     for i in range(1, reps):
@@ -268,6 +296,24 @@
         return remote(ring_out, ring_in.at[i], ring_ss.at[i], ring_rs.at[i], ring_peer(i))
 
     to_peers(ring_copy, sections)
+    for s in (1, 0):
+        far, near = (3, 5) if s == 1 else (2, 4)
+        p_copy(far).wait_recv()
+        p_copy(near).wait_recv()
+        psend[6 + s] = (
+            kept[s] + precv[far].astype(jnp.float32) + precv[near].astype(jnp.float32)
+        ).astype(jnp.bfloat16)
+        if s == 1:
+            p_copy(7).start()
+
+    @pl.when(r != 0)
+    def _():
+        p_copy(6).start()
+
+    @pl.when(r == 0)
+    def _():
+        own_p.start()
+
     for i in range(1, sections):
         ring_copy(i).wait_recv()
         part = part + ring_in[i]
@@ -280,19 +326,14 @@
 
     @pl.when(r != 0)
     def _():
-        p_copy(0).wait_recv()
+        p_copy(6).wait_recv()
 
     @pl.when(r == 0)
     def _():
         own_p.wait()
 
-    def gather(j, summed):
-        p_copy(j).wait_recv()
-        return summed + precv[j].astype(jnp.float32)
-
-    summed = precv[0].astype(jnp.float32)
-    for j in range(1, sections):
-        summed = gather(j, summed)
+    p_copy(7).wait_recv()
+    summed = precv[6].astype(jnp.float32) + precv[7].astype(jnp.float32)
     hsend[...] = summed.T.reshape(hsend.shape)
 
     def h_copy(i):
@@ -324,12 +365,16 @@
 
     @pl.when(r != 0)
     def _():
-        x_copy(0).wait_send()
-        p_copy(0).wait_send()
-
+        x_copy(0, 0).wait_send()
+        p_copy(6).wait_send()
+
+    x_copy(0, 1).wait_send()
+    for g in range(1, 4):
+        x_copy(g, 0).wait_send()
+        x_copy(g, 1).wait_send()
+    for at in (0, 1, 2, 3, 4, 5, 7):
+        p_copy(at).wait_send()
     for j in range(1, sections):
-        x_copy(j).wait_send()
-        p_copy(j).wait_send()
         ring_copy(j).wait_send()
     for i in range(1, reps):
         y_copy(i).wait_send()
@@ -348,9 +393,8 @@
     hid = weight.shape[1]
     share = rows // reps
     wshare = feat // reps
-    adjacency = dense_adjacency(
-        tile_vals[0, 0], tile_pos[0, 0], tile_count[0, 0], rows // tile_vals.shape[-1]
-    )
+    blocks = rows // tile_vals.shape[-1]
+    codes = slot_codes(tile_pos[0, 0], tile_count[0, 0], blocks * blocks)
     bf, fl = jnp.bfloat16, jnp.float32
     sems = [sections] * 2 + [reps] * 4 + [sections] * 2 + [reps] * 4 + [sections] * 2 + [reps] * 4
     act, feat_grad, weight_grad = pl.pallas_call(
@@ -360,14 +404,17 @@
             jax.ShapeDtypeStruct((share, feat), bf),
             jax.ShapeDtypeStruct((feat, hid), fl),
         ),
-        in_specs=[pl.BlockSpec(memory_space=pltpu.VMEM)] * 4,
+        in_specs=[pl.BlockSpec(memory_space=pltpu.VMEM)] * 3
+        + [pl.BlockSpec(memory_space=pltpu.SMEM), pl.BlockSpec(memory_space=pltpu.VMEM)],
         out_specs=[pl.BlockSpec(memory_space=pltpu.VMEM)] * 3,
         scratch_shapes=[
+            pltpu.VMEM((sections, rows, rows), bf),
             pltpu.VMEM((sections, rows, feat), bf),
             pltpu.VMEM((rows, feat), fl),
             pltpu.VMEM((reps, share, feat), fl),
             pltpu.VMEM((reps, share, feat), fl),
             pltpu.VMEM((reps, share, feat), bf),
+            pltpu.VMEM((2, feat, rows), fl),
             pltpu.VMEM((sections, feat, rows), bf),
             pltpu.VMEM((sections, feat, rows), bf),
             pltpu.VMEM((reps, share, feat), fl),
@@ -384,7 +431,7 @@
         compiler_params=pltpu.CompilerParams(
             collective_id=0, has_side_effects=True, vmem_limit_bytes=48 << 20
         ),
-    )(features, weight, adjacency, cotangent)
+    )(features, weight, tile_vals[0, 0], codes, cotangent)
     return (act, feat_grad, weight_grad)
 
 

time: 146 us -> 99.7 us (0.68)
  the two profiles are of different devices: /device:TPU:56 before, /device:TPU:1 now
where the time goes in v3:
time: 99.7 us; the launch traced here: 99.4 us
  Pallas kernels  90.9 us (91%)
  local copies, waits for them, and re-layouts  7.03 us (7%)
    pallas_call x1, Pallas kernels, local(): pl.pallas_call(functools.partial(layer_kernel, blks, reps), out_shape=(ja...  90.9 us
    unnamed x11, local copies, waits for them, and re-layouts  6.26 us

profile of v3, /device:TPU:1, one launch (start us, length us, event | category | flops | bytes accessed | tf_op | source)
XLA Modules:
  0.0 99.4 jit_solution(5203418146962568316)
XLA Ops:
  0.6 0.7 iota_compare_fusion.1
  1.3 0.8 copy.9
  2.1 0.1 select_reduce_fusion.code_ref
  2.2 0.0 copy-start
  2.2 1.9 %copy-done = bf16[1,1,8,12,128,128]{5,4,3,2,1,0:T(8,128)(2,1)S(1)} copy-done((bf16[1,1,8,12,128,128]{5,4,3,2,1,0:T(8,128)(2,1)S(1)}, bf16[1,1,8,12,128,128]{5,4,3,2,1,0:T(8,128)(2,1)}, u32[]{:S(2)}) %copy-start) | copy-done | bytes 3145752
  4.1 0.0 copy-start.1
  4.1 0.9 copy-done.1
  5.0 0.0 copy-start.2
  5.0 0.8 copy-done.2
  5.8 0.0 copy-start.3
  5.8 0.8 copy-done.3
  6.6 90.9 %shard_map.85 = (bf16[64,256]{1,0:T(8,128)(2,1)S(1)}, bf16[64,128]{1,0:T(8,128)(2,1)S(1)}, f32[128,256]{1,0:T(8,128)S(1)}) custom-call(bf16[512,128]{1,0:T(8,128)(2,1)S(1)} %copy-done.1, bf16[128,256]{1,0:T(8,128)(2,1)S(1)} %copy-done.2, bf16[8,12,128,128]{3,2,1,0:T(8,128)(2,1)S(1)} %bitcast.3, s32[8,16]{1,0:T(8,128)S(1)} %select_reduce_fusion.code_ref, ...), custom_call_target="tpu_custom_call" | custom-call | tf_op jit(solution)/shard_map/pallas_call | solution.py:400
  97.5 0.6 copy.13
  98.1 0.6 copy.14
  98.7 0.7 copy.15
  (1 shorter events, 0.0 us)
Async XLA Ops:
  2.2 1.9 %copy-start = (bf16[1,1,8,12,128,128]{5,4,3,2,1,0:T(8,128)(2,1)S(1)}, bf16[1,1,8,12,128,128]{5,4,3,2,1,0:T(8,128)(2,1)}, u32[]{:S(2)}) copy-start(bf16[1,1,8,12,128,128]{5,4,3,2,1,0:T(8,128)(2,1)} %param.8) | copy-start | bytes 9437188
  4.1 0.9 copy-start.1
  5.0 0.8 copy-start.2
  5.8 0.8 copy-start.3

commit v4 on v3

v4 whole, which is shorter than its diff:
```python
import functools
import math

import jax
import jax.numpy as jnp
from jax import lax
from jax.experimental import pallas as pl
from jax.experimental.pallas import tpu as pltpu
from jax.sharding import PartitionSpec as P

MESH = pl.DeviceIdType.MESH


def slot_codes(positions, counts, cells):
    slots = jnp.arange(positions.shape[1], dtype=jnp.int32)[None, None, :]
    hits = positions[:, None, :] == jnp.arange(cells, dtype=jnp.int32)[None, :, None]
    hits = hits & (slots < counts[:, None, None])
    return jnp.sum(jnp.where(hits, slots + 1, 0), axis=-1, dtype=jnp.int32)


def gelu_and_slope(value):
    scale = math.sqrt(2.0 / math.pi)
    square = value * value
    bend = jnp.tanh(scale * (value + 0.044715 * (square * value)))
    half = 0.5 * (1.0 + bend)
    slope = half + 0.5 * value * (1.0 - bend * bend) * (
        scale * (1.0 + 3.0 * 0.044715 * square)
    )
    return value * half, slope


def dot(left, right, contract=(1, 0)):
    return lax.dot_general(
        left,
        right,
        (((contract[0],), (contract[1],)), ((), ())),
        preferred_element_type=jnp.float32,
    )


def layer_kernel(
    blks,
    reps,
    features_ref,
    weight_ref,
    tiles_ref,
    code_ref,
    cot_ref,
    act_ref,
    feat_ref,
    wgrad_ref,
    adj_ref,
    xs,
    total,
    ysend,
    yrecv,
    urows,
    kept,
    psend,
    precv,
    hsend,
    hrecv,
    wsend,
    wrecv,
    q_out,
    q_in,
    z_out,
    z_in,
    wall,
    x_ss,
    x_rs,
    y_ss,
    y_rs,
    u_ss,
    u_rs,
    p_ss,
    p_rs,
    h_ss,
    h_rs,
    w_ss,
    w_rs,
    q_ss,
    q_rs,
    z_ss,
    z_rs,
    g_ss,
    g_rs,
):
    b = lax.axis_index("blk")
    r = lax.axis_index("rep")
    sections = blks // reps
    share = cot_ref.shape[0]
    rows = features_ref.shape[0]

    span = 2 * reps
    turns = sections // 2
    z = lax.div(b, span)
    q = lax.rem(b, span)

    def ahead(s):
        return (z * span + lax.rem(q + r + reps * s, span), r)

    def behind(s):
        return (z * span + lax.rem(q - r - reps * s + 2 * span, span), r)

    up = (lax.rem(z + 1, turns) * span + q, r)
    down = (lax.rem(z + turns - 1, turns) * span + q, r)

    def section_of(g, s):
        wrapped = (q - r - reps * s < 0).astype(jnp.int32)
        return lax.rem(2 * (g - wrapped) + s + sections, sections)

    def rep_peer(i):
        return (b, lax.rem(r + i, reps))

    def q_peer(i):
        return (z * span + lax.rem(q + i, span), r)

    def z_peer(i):
        return (lax.rem(z + i, turns) * span + q, r)

    def remote(src, dst, ss, rs, device):
        return pltpu.make_async_remote_copy(
            src_ref=src,
            dst_ref=dst,
            send_sem=ss,
            recv_sem=rs,
            device_id=device,
            device_id_type=MESH,
        )

    barrier = pltpu.get_barrier_semaphore()

    def greet(device):
        pl.semaphore_signal(barrier, inc=1, device_id=device, device_id_type=MESH)

    @pl.when(r != 0)
    def _():
        greet(ahead(0))
        greet(behind(0))

    greet(ahead(1))
    greet(behind(1))
    greet(up)
    greet(down)
    for i in range(1, turns):
        greet(z_peer(i))
    for i in range(1, span):
        greet(q_peer(i))
    for i in range(1, reps):
        greet(rep_peer(i))
    greeted = 4 + (turns - 1) + (span - 1) + (reps - 1)
    pl.semaphore_wait(barrier, jnp.where(r == 0, greeted, greeted + 2))

    part_rows = rows // 2

    def x_copy(g, s, c):
        at = 2 * g + s
        piece = pl.ds(c * part_rows, part_rows)
        if g == 0:
            source, device = features_ref, ahead(s)
        elif g == 1:
            source, device = xs.at[s], up
        elif g == 3:
            source, device = xs.at[s], down
        else:
            source, device = xs.at[2 if s == 0 else 7], (up if s == 0 else down)
        return remote(
            source.at[piece], xs.at[at, piece], x_ss.at[at, c], x_rs.at[at, c], device
        )

    def own_x(c):
        piece = pl.ds(c * part_rows, part_rows)
        return pltpu.make_async_copy(features_ref.at[piece], xs.at[0, piece], x_rs.at[0, c])

    for c in range(2):

        @pl.when(r != 0)
        def _():
            x_copy(0, 0, c).start()

        @pl.when(r == 0)
        def _():
            own_x(c).start()

        x_copy(0, 1, c).start()

    tile = tiles_ref.shape[-1]
    blocks = rows // tile

    def place(j, carry):
        for n in range(blocks):
            for m in range(blocks):
                code = code_ref[j, n * blocks + m]
                picked = tiles_ref[j, jnp.maximum(code - 1, 0)]
                adj_ref[j, n * tile : (n + 1) * tile, m * tile : (m + 1) * tile] = jnp.where(
                    code > 0, picked, jnp.zeros_like(picked)
                )
        return carry

    lax.fori_loop(0, sections, place, 0)

    def term(g, s):
        return dot(adj_ref[section_of(g, s)], xs[2 * g + s])

    for c in range(2):

        @pl.when(r != 0)
        def _():
            x_copy(0, 0, c).wait_recv()

        @pl.when(r == 0)
        def _():
            own_x(c).wait()

        x_copy(1, 0, c).start()
        x_copy(3, 0, c).start()
        x_copy(0, 1, c).wait_recv()
        x_copy(3, 1, c).start()
        x_copy(1, 1, c).start()

    total[...] = term(0, 0) + term(0, 1)
    for c in range(2):
        x_copy(1, 0, c).wait_recv()
        x_copy(2, 0, c).start()
        x_copy(3, 1, c).wait_recv()
        x_copy(2, 1, c).start()
    total[...] += term(1, 0) + term(3, 1)
    for g, s in ((3, 0), (1, 1), (2, 0), (2, 1)):
        x_copy(g, s, 0).wait_recv()
        x_copy(g, s, 1).wait_recv()
        total[...] += term(g, s)

    ysend[...] = total[...].astype(jnp.bfloat16).reshape(ysend.shape)

    def to_peers(copy, count):
        for i in range(1, count):
            copy(i).start()

    def take(copy, count):
        for i in range(1, count):
            copy(i).wait_recv()

    def y_copy(i):
        peer = rep_peer(i)
        return remote(ysend.at[peer[1]], yrecv.at[i], y_ss.at[i], y_rs.at[i], peer)

    to_peers(y_copy, reps)
    mixed = ysend[r].astype(jnp.float32)
    for i in range(1, reps):
        y_copy(i).wait_recv()
        mixed = mixed + yrecv[i].astype(jnp.float32)

    weight = weight_ref[...]
    high = mixed.astype(jnp.bfloat16)
    low = (mixed - high.astype(jnp.float32)).astype(jnp.bfloat16)
    act, slope = gelu_and_slope(dot(high, weight) + dot(low, weight))
    act_ref[...] = act.astype(jnp.bfloat16)
    pre_grad = (cot_ref[...].astype(jnp.float32) * slope).astype(jnp.bfloat16)
    urows[r] = dot(pre_grad, weight, (1, 1)).astype(jnp.bfloat16)

    def u_copy(i):
        return remote(urows.at[r], urows.at[r], u_ss.at[i], u_rs.at[i], rep_peer(i))

    def u_arrival(i):
        source = lax.rem(r - i + reps, reps)
        return remote(urows.at[source], urows.at[source], u_ss.at[i], u_rs.at[i], rep_peer(i))

    to_peers(u_copy, reps)
    wsend[...] = dot(high, pre_grad, (0, 0)).reshape(wsend.shape)

    def w_copy(i):
        peer = rep_peer(i)
        return remote(wsend.at[peer[1]], wrecv.at[i], w_ss.at[i], w_rs.at[i], peer)

    to_peers(w_copy, reps)
    take(u_arrival, reps)
    flipped = urows[...].reshape(rows, urows.shape[2]).T

    def p_copy(at, c):
        device = (down, up, down, down, up, up, behind(0), behind(1))[at]
        return remote(psend.at[at, c], precv.at[at, c], p_ss.at[at, c], p_rs.at[at, c], device)

    def own_p(c):
        return pltpu.make_async_copy(psend.at[6, c], precv.at[6, c], p_rs.at[6, c])

    def back(g, s):
        return dot(flipped, adj_ref[section_of(g, s)])

    def half(value, c):
        return value[:, c * part_rows : (c + 1) * part_rows]

    def arrived(at, c):
        p_copy(at, c).wait_recv()
        return precv[at, c].astype(jnp.float32)

    for pair in (((0, 2, 0), (1, 2, 1)), ((3, 1, 1), (4, 3, 0))):
        for at, g, s in pair:
            value = back(g, s).astype(jnp.bfloat16)
            psend[at, 0] = half(value, 0)
            psend[at, 1] = half(value, 1)
            p_copy(at, 0).start()
            p_copy(at, 1).start()
    for at, g, s in ((0, 0, 0), (1, 0, 1), (2, 1, 0), (3, 3, 1)):
        kept[at] = back(g, s)

    part = wsend[r]
    for i in range(1, reps):
        w_copy(i).wait_recv()
        part = part + wrecv[i]
    q_out[...] = part

    def q_copy(i):
        return remote(q_out, q_in.at[i], q_ss.at[i], q_rs.at[i], q_peer(i))

    to_peers(q_copy, span)

    for c in range(2):
        for near, at in ((0, 2), (1, 5)):
            mine = half(kept[2 + near], c)
            psend[at, c] = (mine + arrived(near, c)).astype(jnp.bfloat16)
            p_copy(at, c).start()

    for i in range(1, span):
        q_copy(i).wait_recv()
        part = part + q_in[i]
    z_out[...] = part

    def z_copy(i):
        return remote(z_out, z_in.at[i], z_ss.at[i], z_rs.at[i], z_peer(i))

    to_peers(z_copy, turns)

    for c in range(2):
        psend[7, c] = (half(kept[1], c) + arrived(3, c) + arrived(5, c)).astype(jnp.bfloat16)
        p_copy(7, c).start()
        psend[6, c] = (half(kept[0], c) + arrived(2, c) + arrived(4, c)).astype(jnp.bfloat16)

        @pl.when(r != 0)
        def _():
            p_copy(6, c).start()

        @pl.when(r == 0)
        def _():
            own_p(c).start()

    for i in range(1, turns):
        z_copy(i).wait_recv()
        part = part + z_in[i]
    wall[r] = part

    def g_copy(i):
        return remote(wall.at[r], wall.at[r], g_ss.at[i], g_rs.at[i], rep_peer(i))

    def g_arrival(i):
        source = lax.rem(r - i + reps, reps)
        return remote(wall.at[source], wall.at[source], g_ss.at[i], g_rs.at[i], rep_peer(i))

    to_peers(g_copy, reps)

    def owned(c):
        @pl.when(r != 0)
        def _():
            p_copy(6, c).wait_recv()

        @pl.when(r == 0)
        def _():
            own_p(c).wait()

        return precv[6, c].astype(jnp.float32) + arrived(7, c)

    for c in range(2):
        kept[0, :, c * part_rows : (c + 1) * part_rows] = owned(c)
    summed = kept[0]
    hsend[...] = summed.T.astype(jnp.bfloat16).reshape(hsend.shape)

    def h_copy(i):
        peer = rep_peer(i)
        return remote(hsend.at[peer[1]], hrecv.at[i], h_ss.at[i], h_rs.at[i], peer)

    to_peers(h_copy, reps)
    rows_grad = hsend[r].astype(jnp.float32)
    for i in range(1, reps):
        h_copy(i).wait_recv()
        rows_grad = rows_grad + hrecv[i].astype(jnp.float32)
    feat_ref[...] = rows_grad.astype(jnp.bfloat16)
    take(g_arrival, reps)
    wgrad_ref[...] = wall[...].reshape(wgrad_ref.shape)

    for c in range(2):

        @pl.when(r != 0)
        def _():
            x_copy(0, 0, c).wait_send()
            p_copy(6, c).wait_send()

        x_copy(0, 1, c).wait_send()
        for g in range(1, 4):
            x_copy(g, 0, c).wait_send()
            x_copy(g, 1, c).wait_send()
        for at in (0, 1, 2, 3, 4, 5, 7):
            p_copy(at, c).wait_send()
    for i in range(1, turns):
        z_copy(i).wait_send()
    for i in range(1, span):
        q_copy(i).wait_send()
    for i in range(1, reps):
        y_copy(i).wait_send()
        u_copy(i).wait_send()
        w_copy(i).wait_send()
        h_copy(i).wait_send()
        g_copy(i).wait_send()


def local(features, weight, tile_vals, tile_pos, tile_count, cotangent):
    reps = lax.axis_size("rep")
    blks = lax.axis_size("blk")
    sections = blks // reps
    rows, feat = features.shape
    hid = weight.shape[1]
    share = rows // reps
    wshare = feat // reps
    blocks = rows // tile_vals.shape[-1]
    codes = slot_codes(tile_pos[0, 0], tile_count[0, 0], blocks * blocks)
    bf, fl = jnp.bfloat16, jnp.float32
    span, turns = 2 * reps, sections // 2
    halves = (sections, 2)
    sems = [halves] * 2 + [(reps,)] * 4 + [halves] * 2 + [(reps,)] * 4
    sems += [(span,)] * 2 + [(turns,)] * 2 + [(reps,)] * 2
    act, feat_grad, weight_grad = pl.pallas_call(
        functools.partial(layer_kernel, blks, reps),
        out_shape=(
            jax.ShapeDtypeStruct((share, hid), bf),
            jax.ShapeDtypeStruct((share, feat), bf),
            jax.ShapeDtypeStruct((feat, hid), fl),
        ),
        in_specs=[pl.BlockSpec(memory_space=pltpu.VMEM)] * 3
        + [pl.BlockSpec(memory_space=pltpu.SMEM), pl.BlockSpec(memory_space=pltpu.VMEM)],
        out_specs=[pl.BlockSpec(memory_space=pltpu.VMEM)] * 3,
        scratch_shapes=[
            pltpu.VMEM((sections, rows, rows), bf),
            pltpu.VMEM((sections, rows, feat), bf),
            pltpu.VMEM((rows, feat), fl),
            pltpu.VMEM((reps, share, feat), bf),
            pltpu.VMEM((reps, share, feat), bf),
            pltpu.VMEM((reps, share, feat), bf),
            pltpu.VMEM((4, feat, rows), fl),
            pltpu.VMEM((sections, 2, feat, rows // 2), bf),
            pltpu.VMEM((sections, 2, feat, rows // 2), bf),
            pltpu.VMEM((reps, share, feat), bf),
            pltpu.VMEM((reps, share, feat), bf),
            pltpu.VMEM((reps, wshare, hid), fl),
            pltpu.VMEM((reps, wshare, hid), fl),
            pltpu.VMEM((wshare, hid), fl),
            pltpu.VMEM((span, wshare, hid), fl),
            pltpu.VMEM((wshare, hid), fl),
            pltpu.VMEM((turns, wshare, hid), fl),
            pltpu.VMEM((reps, wshare, hid), fl),
        ]
        + [pltpu.SemaphoreType.DMA(shape) for shape in sems],
        compiler_params=pltpu.CompilerParams(
            collective_id=0, has_side_effects=True, vmem_limit_bytes=48 << 20
        ),
    )(features, weight, tile_vals[0, 0], codes, cotangent)
    return (act, feat_grad, weight_grad)


def solution(mesh):
    placed = (
        P("blk", None),
        P(),
        P("blk", "rep", None, None, None, None),
        P("blk", "rep", None, None),
        P("blk", "rep", None),
        P(("blk", "rep"), None),
    )
    return jax.shard_map(
        local,
        mesh=mesh,
        in_specs=placed,
        out_specs=(P(("blk", "rep"), None), P(("blk", "rep"), None), P()),
        check_vma=False,
    )
```

time: 99.7 us -> 90.8 us (0.911)
  Pallas kernels: 90.9 us -> 82 us
    pallas_call x1, Pallas kernels: 90.9 us -> 82 us  [local(): pl.pallas_call(functools.partial(layer_kernel, blks, reps), out_shape=(ja...]
where the time goes in v4:
time: 90.8 us; the launch traced here: 90.5 us
  Pallas kernels  82 us (90%)
  local copies, waits for them, and re-layouts  7.03 us (8%)
    pallas_call x1, Pallas kernels, local(): pl.pallas_call(functools.partial(layer_kernel, blks, reps), out_shape=(ja...  82 us
    unnamed x11, local copies, waits for them, and re-layouts  6.26 us

profile of v4, /device:TPU:1, one launch (start us, length us, event | category | flops | bytes accessed | tf_op | source)
XLA Modules:
  0.0 90.5 jit_solution(11818806485375111453)
XLA Ops:
  0.6 0.7 iota_compare_fusion.1
  1.3 0.8 copy.9
  2.1 0.1 select_reduce_fusion.code_ref
  2.2 0.0 copy-start
  2.2 1.9 %copy-done = bf16[1,1,8,12,128,128]{5,4,3,2,1,0:T(8,128)(2,1)S(1)} copy-done((bf16[1,1,8,12,128,128]{5,4,3,2,1,0:T(8,128)(2,1)S(1)}, bf16[1,1,8,12,128,128]{5,4,3,2,1,0:T(8,128)(2,1)}, u32[]{:S(2)}) %copy-start) | copy-done | bytes 3145752
  4.1 0.0 copy-start.1
  4.1 0.9 copy-done.1
  5.0 0.0 copy-start.2
  5.0 0.8 copy-done.2
  5.8 0.0 copy-start.3
  5.8 0.8 copy-done.3
  6.6 82.0 %shard_map.85 = (bf16[64,256]{1,0:T(8,128)(2,1)S(1)}, bf16[64,128]{1,0:T(8,128)(2,1)S(1)}, f32[128,256]{1,0:T(8,128)S(1)}) custom-call(bf16[512,128]{1,0:T(8,128)(2,1)S(1)} %copy-done.1, bf16[128,256]{1,0:T(8,128)(2,1)S(1)} %copy-done.2, bf16[8,12,128,128]{3,2,1,0:T(8,128)(2,1)S(1)} %bitcast.3, s32[8,16]{1,0:T(8,128)S(1)} %select_reduce_fusion.code_ref, ...), custom_call_target="tpu_custom_call" | custom-call | tf_op jit(solution)/shard_map/pallas_call | solution.py:430
  88.6 0.6 copy.13
  89.2 0.6 copy.14
  89.8 0.7 copy.15
  (1 shorter events, 0.0 us)
Async XLA Ops:
  2.2 1.9 %copy-start = (bf16[1,1,8,12,128,128]{5,4,3,2,1,0:T(8,128)(2,1)S(1)}, bf16[1,1,8,12,128,128]{5,4,3,2,1,0:T(8,128)(2,1)}, u32[]{:S(2)}) copy-start(bf16[1,1,8,12,128,128]{5,4,3,2,1,0:T(8,128)(2,1)} %param.8) | copy-start | bytes 9437188
  4.1 0.9 copy-start.1
  5.0 0.8 copy-start.2
  5.8 0.8 copy-start.3

commit v5 on v4

--- a/solution.py
+++ b/solution.py
@@ -42,13 +42,16 @@
     blks,
     reps,
     features_ref,
-    weight_ref,
-    tiles_ref,
+    weight_hbm,
+    tiles_hbm,
     code_ref,
-    cot_ref,
+    cot_hbm,
     act_ref,
     feat_ref,
     wgrad_ref,
+    weight_ref,
+    tiles_ref,
+    cot_ref,
     adj_ref,
     xs,
     total,
@@ -67,6 +70,7 @@
     z_out,
     z_in,
     wall,
+    load_sems,
     x_ss,
     x_rs,
     y_ss,
@@ -129,6 +133,15 @@
             device_id_type=MESH,
         )
 
+    loads = [
+        pltpu.make_async_copy(source, target, load_sems.at[i])
+        for i, (source, target) in enumerate(
+            ((tiles_hbm, tiles_ref), (weight_hbm, weight_ref), (cot_hbm, cot_ref))
+        )
+    ]
+    for load in loads:
+        load.start()
+
     barrier = pltpu.get_barrier_semaphore()
 
     def greet(device):
@@ -198,7 +211,10 @@
                 )
         return carry
 
+    loads[0].wait()
     lax.fori_loop(0, sections, place, 0)
+    loads[1].wait()
+    loads[2].wait()
 
     def term(g, s):
         return dot(adj_ref[section_of(g, s)], xs[2 * g + s])
@@ -425,7 +441,7 @@
     bf, fl = jnp.bfloat16, jnp.float32
     span, turns = 2 * reps, sections // 2
     halves = (sections, 2)
-    sems = [halves] * 2 + [(reps,)] * 4 + [halves] * 2 + [(reps,)] * 4
+    sems = [(3,)] + [halves] * 2 + [(reps,)] * 4 + [halves] * 2 + [(reps,)] * 4
     sems += [(span,)] * 2 + [(turns,)] * 2 + [(reps,)] * 2
     act, feat_grad, weight_grad = pl.pallas_call(
         functools.partial(layer_kernel, blks, reps),
@@ -434,10 +450,13 @@
             jax.ShapeDtypeStruct((share, feat), bf),
             jax.ShapeDtypeStruct((feat, hid), fl),
         ),
-        in_specs=[pl.BlockSpec(memory_space=pltpu.VMEM)] * 3
-        + [pl.BlockSpec(memory_space=pltpu.SMEM), pl.BlockSpec(memory_space=pltpu.VMEM)],
+        in_specs=[pl.BlockSpec(memory_space=pltpu.HBM)] * 3
+        + [pl.BlockSpec(memory_space=pltpu.SMEM), pl.BlockSpec(memory_space=pltpu.HBM)],
         out_specs=[pl.BlockSpec(memory_space=pltpu.VMEM)] * 3,
         scratch_shapes=[
+            pltpu.VMEM(weight.shape, bf),
+            pltpu.VMEM(tile_vals.shape[2:], bf),
+            pltpu.VMEM(cotangent.shape, bf),
             pltpu.VMEM((sections, rows, rows), bf),
             pltpu.VMEM((sections, rows, feat), bf),
             pltpu.VMEM((rows, feat), fl),
@@ -459,7 +478,7 @@
         ]
         + [pltpu.SemaphoreType.DMA(shape) for shape in sems],
         compiler_params=pltpu.CompilerParams(
-            collective_id=0, has_side_effects=True, vmem_limit_bytes=48 << 20
+            collective_id=0, has_side_effects=True, vmem_limit_bytes=63 << 20
         ),
     )(features, weight, tile_vals[0, 0], codes, cotangent)
     return (act, feat_grad, weight_grad)

time: 90.8 us -> 90.8 us (level)
  local copies, waits for them, and re-layouts: 7.03 us -> 5.03 us
    unnamed x11 -> x3, local copies, waits for them, and re-layouts: 6.26 us -> 4.26 us
where the time goes in v5:
time: 90.8 us; the launch traced here: 89.8 us
  Pallas kernels  82.7 us (91%)
  local copies, waits for them, and re-layouts  5.03 us (6%)
  other arithmetic  1.37 us (2%)
    pallas_call x1, Pallas kernels, local(): pl.pallas_call(functools.partial(layer_kernel, blks, reps), out_shape=(ja...  82.7 us
    unnamed x3, local copies, waits for them, and re-layouts  4.26 us

profile of v5, /device:TPU:1, one launch (start us, length us, event | category | flops | bytes accessed | tf_op | source)
XLA Modules:
  0.0 89.8 jit_solution(9309309644963431799)
XLA Ops:
  0.6 0.7 iota_compare_fusion.1
  1.3 0.8 copy.9
  2.1 0.7 select_reduce_fusion.code_ref
  2.8 82.7 %shard_map.85 = (bf16[64,256]{1,0:T(8,128)(2,1)}, bf16[64,128]{1,0:T(8,128)(2,1)}, f32[128,256]{1,0:T(8,128)}) custom-call(bf16[512,128]{1,0:T(8,128)(2,1)} %features_ref.1, bf16[128,256]{1,0:T(8,128)(2,1)} %weight_hbm.1, bf16[8,12,128,128]{3,2,1,0:T(8,128)(2,1)} %bitcast.3, s32[8,16]{1,0:T(8,128)} %select_reduce_fusion.code_ref, bf16[64,256]{1,0:T(8,128)(2,1)} %cot_hbm.1), custom_call_target="tpu_custom_call" | custom-call | tf_op jit(solution)/shard_map/pallas_call | solution.py:446
  85.5 1.4 %copy.13 = bf16[64,256]{1,0:T(8,128)(2,1)} copy(bf16[64,256]{1,0:T(8,128)(2,1)} %get-tuple-element.6) | data formatting | bytes 65536
  86.9 1.3 %copy.14 = bf16[64,128]{1,0:T(8,128)(2,1)} copy(bf16[64,128]{1,0:T(8,128)(2,1)} %get-tuple-element.7) | data formatting | bytes 32768
  88.2 1.6 %copy.15 = f32[128,256]{1,0:T(8,128)} copy(f32[128,256]{1,0:T(8,128)} %get-tuple-element.8) | data formatting | bytes 262144
  (1 shorter events, 0.0 us)

commit v6 on v5

--- a/solution.py
+++ b/solution.py
@@ -478,7 +478,7 @@
         ]
         + [pltpu.SemaphoreType.DMA(shape) for shape in sems],
         compiler_params=pltpu.CompilerParams(
-            collective_id=0, has_side_effects=True, vmem_limit_bytes=63 << 20
+            collective_id=0, has_side_effects=True, vmem_limit_bytes=53 << 20
         ),
     )(features, weight, tile_vals[0, 0], codes, cotangent)
     return (act, feat_grad, weight_grad)

time: 90.8 us -> 89 us (0.980)
    unnamed x3 -> x9, local copies, waits for them, and re-layouts: 4.26 us -> 4.37 us
where the time goes in v6:
time: 89 us; the launch traced here: 88.7 us
  Pallas kernels  82.1 us (92%)
  local copies, waits for them, and re-layouts  5.14 us (6%)
    pallas_call x1, Pallas kernels, local(): pl.pallas_call(functools.partial(layer_kernel, blks, reps), out_shape=(ja...  82.1 us
    unnamed x9, local copies, waits for them, and re-layouts  4.37 us

profile of v6, /device:TPU:1, one launch (start us, length us, event | category | flops | bytes accessed | tf_op | source)
XLA Modules:
  0.0 88.7 jit_solution(13850500345062889651)
XLA Ops:
  0.6 0.7 iota_compare_fusion.1
  1.3 0.8 copy.9
  2.1 0.1 select_reduce_fusion.code_ref
  2.2 0.0 copy-start
  2.2 0.9 %copy-done = bf16[512,128]{1,0:T(8,128)(2,1)S(1)} copy-done((bf16[512,128]{1,0:T(8,128)(2,1)S(1)}, bf16[512,128]{1,0:T(8,128)(2,1)}, u32[]{:S(2)}) %copy-start) | copy-done | bytes 131096
  3.1 0.0 copy-start.1
  3.1 0.8 copy-done.1
  3.9 0.0 copy-start.2
  3.9 0.8 copy-done.2
  4.7 82.1 %shard_map.85 = (bf16[64,256]{1,0:T(8,128)(2,1)S(1)}, bf16[64,128]{1,0:T(8,128)(2,1)S(1)}, f32[128,256]{1,0:T(8,128)S(1)}) custom-call(bf16[512,128]{1,0:T(8,128)(2,1)S(1)} %copy-done, bf16[128,256]{1,0:T(8,128)(2,1)S(1)} %copy-done.1, bf16[8,12,128,128]{3,2,1,0:T(8,128)(2,1)} %bitcast.3, s32[8,16]{1,0:T(8,128)S(1)} %select_reduce_fusion.code_ref, ...), custom_call_target="tpu_custom_call" | custom-call | tf_op jit(solution)/shard_map/pallas_call | solution.py:446
  86.8 0.6 copy.13
  87.4 0.6 copy.14
  88.0 0.7 copy.15
  (1 shorter events, 0.0 us)
Async XLA Ops:
  2.2 0.9 %copy-start = (bf16[512,128]{1,0:T(8,128)(2,1)S(1)}, bf16[512,128]{1,0:T(8,128)(2,1)}, u32[]{:S(2)}) copy-start(bf16[512,128]{1,0:T(8,128)(2,1)} %features_ref.1) | copy-start | bytes 393220
  3.1 0.8 copy-start.1
  3.9 0.8 copy-start.2
